TPU v7x, 512 devices: a whole 4x8x8 slice. The times are simulated.
512 devices in a mesh: lon: 32 (over z, x), lat: 16 (over y, core).
Axes of the slice: x: 4, y: 8, z: 8, core: 2. Of those that a mesh axis runs over, the one named last changes fastest.
Arguments:
- right_side: float32 [2, 32, 256, 4096], P(None, None, 'lat', 'lon'), may hold values from -36 to 36
- sea_mask: int32 [32, 256, 4096], P(None, 'lat', 'lon'), may hold values 0 or 1
- levels: int32 [256, 4096], P('lat', 'lon'), may hold values from 0 to 32
- east_diffusivity: bfloat16 [32, 256, 4096], P(None, 'lat', 'lon'), may hold values from 1 to 8
- north_diffusivity: bfloat16 [32, 256, 4096], P(None, 'lat', 'lon'), may hold values from 1 to 8
- vertical_diffusivity: bfloat16 [32, 256, 4096], P(None, 'lat', 'lon'), may hold values from 0.5 to 8
Outputs:
- solution_field: float32 [2, 32, 256, 4096], P(None, None, 'lat', 'lon')
- residual: float32 [2, 32, 256, 4096], P(None, None, 'lat', 'lon')
All inputs are finite; a program needn't handle non-finite values. No bound on the sum of `sea_mask` on one device may be relied on, other than what follows from the above.
Results may differ from a plain program's by a relative error of at most 0.004.
Values sent between devices are 32-bit elements; how exact they have to be, the bound alone decides.
A program may use at most 64 MiB of HBM per device.

v0:
```python
import jax
import jax.numpy as jnp
from jax import lax
from jax.sharding import PartitionSpec as P

ITERS = 2


def from_behind(x, axis, by):
    devices = lax.axis_size(axis)
    return lax.ppermute(x, axis, [(i, (i + by) % devices) for i in range(devices)])


def shifted(x, axis, by):
    devices = lax.axis_size(axis)
    pairs = [(i, i + by) for i in range(devices) if 0 <= i + by < devices]
    return lax.ppermute(x, axis, pairs)


def local_sum(first, second):
    return jnp.sum(first * second, axis=(1, 2, 3))


def expand(scalars):
    return scalars[:, None, None, None]


def vertical_change(field, coef_down):
    value_below = jnp.concatenate([field[:, 1:], jnp.zeros_like(field[:, :1])], axis=1)
    flux_down = coef_down * (value_below - field)
    flux_above = jnp.concatenate([jnp.zeros_like(flux_down[:, :1]), flux_down[:, :-1]], axis=1)
    return flux_above - flux_down


def body(right_side, sea_mask, levels, east_diffusivity, north_diffusivity, vertical_diffusivity):
    depth_index = lax.broadcasted_iota(jnp.int32, sea_mask.shape, 0)
    ocean_flag = ((sea_mask == 1) & (depth_index < levels[None])).astype(jnp.int32)
    east_column = from_behind(ocean_flag[:, :, :1], "lon", -1)
    north_row = shifted(ocean_flag[:, :1, :], "lat", -1)
    ocean = ocean_flag.astype(jnp.float32)
    ocean_east = jnp.concatenate([ocean[:, :, 1:], east_column.astype(jnp.float32)], axis=2)
    ocean_north = jnp.concatenate([ocean[:, 1:, :], north_row.astype(jnp.float32)], axis=1)
    ocean_below = jnp.concatenate([ocean[1:], jnp.zeros_like(ocean[:1])], axis=0)
    coef_east = east_diffusivity.astype(jnp.float32) * ocean * ocean_east
    coef_north = north_diffusivity.astype(jnp.float32) * ocean * ocean_north
    coef_down = vertical_diffusivity.astype(jnp.float32) * ocean * ocean_below
    solution = jnp.zeros_like(right_side)
    residual = right_side

    def sum_squares(field):
        return lax.psum(local_sum(field, field), ("lon", "lat"))

    direction = right_side
    norm_now = sum_squares(residual)
    for iteration in range(ITERS):
        first_column = from_behind(direction[:, :, :, :1], "lon", -1)
        first_row = shifted(direction[:, :, :1, :], "lat", -1)
        value_east = jnp.concatenate([direction[:, :, :, 1:], first_column], axis=3)
        value_north = jnp.concatenate([direction[:, :, 1:, :], first_row], axis=2)
        flux_east = coef_east * (value_east - direction)
        flux_north = coef_north * (value_north - direction)
        last_column = from_behind(flux_east[:, :, :, -1:], "lon", 1)
        last_row = shifted(flux_north[:, :, -1:, :], "lat", 1)
        flux_west = jnp.concatenate([last_column, flux_east[:, :, :, :-1]], axis=3)
        flux_south = jnp.concatenate([last_row, flux_north[:, :, :-1, :]], axis=2)
        image = (
            direction
            + (flux_west - flux_east)
            + (flux_south - flux_north)
            + vertical_change(direction, coef_down)
        )
        step_size = norm_now / lax.psum(local_sum(direction, image), ("lon", "lat"))
        solution = solution + expand(step_size) * direction
        residual = residual - expand(step_size) * image
        norm_next = sum_squares(residual)
        direction = residual + expand(norm_next / norm_now) * direction
        norm_now = norm_next
    return (solution, residual)


def solution(mesh):
    return jax.shard_map(
        body,
        mesh=mesh,
        in_specs=(
            P(None, None, "lat", "lon"),
            P(None, "lat", "lon"),
            P("lat", "lon"),
            P(None, "lat", "lon"),
            P(None, "lat", "lon"),
            P(None, "lat", "lon"),
        ),
        out_specs=(P(None, None, "lat", "lon"), P(None, None, "lat", "lon")),
        check_vma=False,
    )
```

profile of v0, /device:TPU:1, one launch (start us, length us, event | category | flops | bytes accessed | tf_op | source)
XLA Modules:
  0.0 386.5 jit_solution(15036093700359671659)
XLA Ops:
  0.6 1.1 fusion.14
  1.7 8.8 %collective-permute-start.3 = (s32[32,1,128]{2,1,0:T(1,128)S(1)}, s32[32,1,128]{2,1,0:T(1,128)S(1)}, u32[]{:S(2)}, u32[]{:S(2)}) collective-permute-start(s32[32,1,128]{2,1,0:T(1,128)S(1)} %slice.105), channel_id=1, source_target_pairs={{1,0},{2,1},{3,2},{4,3},{5,4},{6,5},{7,6},{8,7},{9,8},{10,9},{11,1... | collective-permute-start | bytes 49160 | tf_op jit(solution)/shard_map/ppermute | solution.py:17
  10.5 7.5 %collective-permute-start = (s32[32,16,1]{2,1,0:T(8,128)S(1)}, s32[32,16,1]{2,1,0:T(8,128)S(1)}, u32[]{:S(2)}, u32[]{:S(2)}) collective-permute-start(s32[32,16,1]{2,1,0:T(8,128)S(1)} %bitcast.13), channel_id=1, source_target_pairs={{0,496},{16,0},{32,16},{48,32},{64,48},{80,64},{96,80},{112,96},{1... | collective-permute-start | bytes 6152 | tf_op jit(solution)/shard_map/ppermute | solution.py:11
  18.1 1.9 collective-permute-start.4
  20.0 2.5 collective-permute-start.1
  22.6 0.2 slice.77
  22.8 0.1 slice.100
  23.0 1.2 collective-permute-done
  24.2 0.2 maximum_multiply_fusion
  24.4 10.9 %collective-permute-done.1 = f32[2,32,16,1]{3,2,1,0:T(8,128)S(1)} collective-permute-done((f32[2,32,16,1]{3,2,1,0:T(8,128)S(1)}, f32[2,32,16,1]{3,2,1,0:T(8,128)S(1)}, u32[]{:S(2)}, u32[]{:S(2)}) %collective-permute-start.1) | collective-permute-done | bytes 4128 | tf_op jit(solution)/shard_map/ppermute | solution.py:11
  35.3 0.4 fusion
  35.7 4.3 %collective-permute-start.5 = (f32[2,32,1,128]{3,2,1,0:T(1,128)S(1)}, f32[2,32,1,128]{3,2,1,0:T(1,128)S(1)}, u32[]{:S(2)}, u32[]{:S(2)}) collective-permute-start(f32[2,32,1,128]{3,2,1,0:T(1,128)S(1)} %slice.106), channel_id=1, source_target_pairs={{0,1},{1,2},{2,3},{3,4},{4,5},{5,6},{6,7},{7,8},{8,9},{9,10},{10,1... | collective-permute-start | bytes 98312 | tf_op jit(solution)/shard_map/ppermute | solution.py:17
  40.0 0.2 slice.102
  40.2 1.9 collective-permute-start.2
  42.2 15.7 %collective-permute-done.2 = f32[2,32,16,1]{3,2,1,0:T(8,128)S(1)} collective-permute-done((f32[2,32,16,1]{3,2,1,0:T(8,128)S(1)}, f32[2,32,16,1]{3,2,1,0:T(8,128)S(1)}, u32[]{:S(2)}, u32[]{:S(2)}) %collective-permute-start.2) | collective-permute-done | bytes 4128 | tf_op jit(solution)/shard_map/ppermute | solution.py:11
  57.9 0.5 multiply_reduce_fusion.2
  58.4 97.2 %all-reduce.5 = (f32[2]{0:T(128)S(1)}, f32[2]{0:T(128)S(1)}) all-reduce(f32[2]{0:T(128)S(1)} %get-tuple-element.3, f32[2]{0:T(128)S(1)} %get-tuple-element.2), channel_id=1, replica_groups=mesh['lon'=32,'lat'=16] {'lon','lat'}, use_global_device_ids=true, to_apply=%region_1.0 | all-reduce | flops 4 | bytes 32 | tf_op jit(solution)/shard_map/psum | solution.py:51
  155.6 0.3 multiply_reduce_fusion.1
  155.9 94.4 %psum.30 = f32[2]{0:T(128)S(1)} all-reduce(f32[2]{0:T(128)S(1)} %multiply_reduce_fusion.1), channel_id=1, replica_groups=mesh['lon'=32,'lat'=16] {'lon','lat'}, use_global_device_ids=true, to_apply=%region_5.0 | all-reduce | flops 2 | bytes 16 | tf_op jit(solution)/shard_map/psum | solution.py:51
  250.3 0.1 multiply_add_fusion.1
  250.5 2.6 collective-permute-start.8
  253.1 4.5 %collective-permute-start.6 = (f32[2,32,16,1]{3,2,1,0:T(8,128)S(1)}, f32[2,32,16,1]{3,2,1,0:T(8,128)S(1)}, u32[]{:S(2)}, u32[]{:S(2)}) collective-permute-start(f32[2,32,16,1]{3,2,1,0:T(8,128)S(1)} %bitcast.8), channel_id=1, source_target_pairs={{0,496},{16,0},{32,16},{48,32},{64,48},{80,64},{96,80},{112,96},{1... | collective-permute-start | bytes 12296 | tf_op jit(solution)/shard_map/ppermute | solution.py:11
  257.7 0.2 slice.110
  257.9 11.3 %collective-permute-done.6 = f32[2,32,16,1]{3,2,1,0:T(8,128)S(1)} collective-permute-done((f32[2,32,16,1]{3,2,1,0:T(8,128)S(1)}, f32[2,32,16,1]{3,2,1,0:T(8,128)S(1)}, u32[]{:S(2)}, u32[]{:S(2)}) %collective-permute-start.6) | collective-permute-done | bytes 4128 | tf_op jit(solution)/shard_map/ppermute | solution.py:11
  269.2 0.4 fusion.5
  269.6 2.6 collective-permute-start.9
  272.2 0.2 slice.112
  272.4 2.8 collective-permute-start.7
  275.3 15.8 %collective-permute-done.7 = f32[2,32,16,1]{3,2,1,0:T(8,128)S(1)} collective-permute-done((f32[2,32,16,1]{3,2,1,0:T(8,128)S(1)}, f32[2,32,16,1]{3,2,1,0:T(8,128)S(1)}, u32[]{:S(2)}, u32[]{:S(2)}) %collective-permute-start.7) | collective-permute-done | bytes 4128 | tf_op jit(solution)/shard_map/ppermute | solution.py:11
  291.1 0.5 multiply_reduce_fusion
  291.6 93.8 %psum.31 = f32[2]{0:T(128)S(1)} all-reduce(f32[2]{0:T(128)S(1)} %get-tuple-element.6), channel_id=1, replica_groups=mesh['lon'=32,'lat'=16] {'lon','lat'}, use_global_device_ids=true, to_apply=%region_7.0 | all-reduce | flops 2 | bytes 16 | tf_op jit(solution)/shard_map/psum | solution.py:72
  385.3 1.2 multiply_subtract_fusion
  (31 shorter events, 0.5 us)
Async XLA Ops:
  0.6 17.4 %copy-start = (f32[2,32,16,128]{3,2,1,0:T(8,128)S(1)}, f32[2,32,16,128]{3,2,1,0:T(8,128)}, u32[]{:S(2)}) copy-start(f32[2,32,16,128]{3,2,1,0:T(8,128)} %param.6) | copy-start | bytes 1572868
  1.7 22.4 %collective-permute-start.3 = (s32[32,1,128]{2,1,0:T(1,128)S(1)}, s32[32,1,128]{2,1,0:T(1,128)S(1)}, u32[]{:S(2)}, u32[]{:S(2)}) collective-permute-start(s32[32,1,128]{2,1,0:T(1,128)S(1)} %slice.105), channel_id=1, source_target_pairs={{1,0},{2,1},{3,2},{4,3},{5,4},{6,5},{7,6},{8,7},{9,8},{10,9},{11,1... | collective-permute-start | bytes 49160 | tf_op jit(solution)/shard_map/ppermute | solution.py:17
  10.5 13.6 %collective-permute-start = (s32[32,16,1]{2,1,0:T(8,128)S(1)}, s32[32,16,1]{2,1,0:T(8,128)S(1)}, u32[]{:S(2)}, u32[]{:S(2)}) collective-permute-start(s32[32,16,1]{2,1,0:T(8,128)S(1)} %bitcast.13), channel_id=1, source_target_pairs={{0,496},{16,0},{32,16},{48,32},{64,48},{80,64},{96,80},{112,96},{1... | collective-permute-start | bytes 6152 | tf_op jit(solution)/shard_map/ppermute | solution.py:11
  18.1 17.2 %collective-permute-start.4 = (f32[2,32,1,128]{3,2,1,0:T(1,128)S(1)}, f32[2,32,1,128]{3,2,1,0:T(1,128)S(1)}, u32[]{:S(2)}, u32[]{:S(2)}) collective-permute-start(f32[2,32,1,128]{3,2,1,0:T(1,128)S(1)} %slice.84), channel_id=1, source_target_pairs={{1,0},{2,1},{3,2},{4,3},{5,4},{6,5},{7,6},{8,7},{9,8},{10,9},{11,1... | collective-permute-start | bytes 98312 | tf_op jit(solution)/shard_map/ppermute | solution.py:17
  20.0 15.3 %collective-permute-start.1 = (f32[2,32,16,1]{3,2,1,0:T(8,128)S(1)}, f32[2,32,16,1]{3,2,1,0:T(8,128)S(1)}, u32[]{:S(2)}, u32[]{:S(2)}) collective-permute-start(f32[2,32,16,1]{3,2,1,0:T(8,128)S(1)} %bitcast.7), channel_id=1, source_target_pairs={{0,496},{16,0},{32,16},{48,32},{64,48},{80,64},{96,80},{112,96},{1... | collective-permute-start | bytes 12296 | tf_op jit(solution)/shard_map/ppermute | solution.py:11
  22.9 1.2 copy-start.1
  23.0 1.2 copy-start.2
  23.0 1.2 copy-start.3
  35.7 22.2 %collective-permute-start.5 = (f32[2,32,1,128]{3,2,1,0:T(1,128)S(1)}, f32[2,32,1,128]{3,2,1,0:T(1,128)S(1)}, u32[]{:S(2)}, u32[]{:S(2)}) collective-permute-start(f32[2,32,1,128]{3,2,1,0:T(1,128)S(1)} %slice.106), channel_id=1, source_target_pairs={{0,1},{1,2},{2,3},{3,4},{4,5},{5,6},{6,7},{7,8},{8,9},{9,10},{10,1... | collective-permute-start | bytes 98312 | tf_op jit(solution)/shard_map/ppermute | solution.py:17
  40.2 17.7 %collective-permute-start.2 = (f32[2,32,16,1]{3,2,1,0:T(8,128)S(1)}, f32[2,32,16,1]{3,2,1,0:T(8,128)S(1)}, u32[]{:S(2)}, u32[]{:S(2)}) collective-permute-start(f32[2,32,16,1]{3,2,1,0:T(8,128)S(1)} %slice.102), channel_id=1, source_target_pairs={{0,16},{16,32},{32,48},{48,64},{64,80},{80,96},{96,112},{112,128},... | collective-permute-start | bytes 12296 | tf_op jit(solution)/shard_map/ppermute | solution.py:11
  250.5 18.8 %collective-permute-start.8 = (f32[2,32,1,128]{3,2,1,0:T(1,128)S(1)}, f32[2,32,1,128]{3,2,1,0:T(1,128)S(1)}, u32[]{:S(2)}, u32[]{:S(2)}) collective-permute-start(f32[2,32,1,128]{3,2,1,0:T(1,128)S(1)} %slice.115), channel_id=1, source_target_pairs={{1,0},{2,1},{3,2},{4,3},{5,4},{6,5},{7,6},{8,7},{9,8},{10,9},{11,1... | collective-permute-start | bytes 98312 | tf_op jit(solution)/shard_map/ppermute | solution.py:17
  253.1 16.2 %collective-permute-start.6 = (f32[2,32,16,1]{3,2,1,0:T(8,128)S(1)}, f32[2,32,16,1]{3,2,1,0:T(8,128)S(1)}, u32[]{:S(2)}, u32[]{:S(2)}) collective-permute-start(f32[2,32,16,1]{3,2,1,0:T(8,128)S(1)} %bitcast.8), channel_id=1, source_target_pairs={{0,496},{16,0},{32,16},{48,32},{64,48},{80,64},{96,80},{112,96},{1... | collective-permute-start | bytes 12296 | tf_op jit(solution)/shard_map/ppermute | solution.py:11
  269.6 21.5 %collective-permute-start.9 = (f32[2,32,1,128]{3,2,1,0:T(1,128)S(1)}, f32[2,32,1,128]{3,2,1,0:T(1,128)S(1)}, u32[]{:S(2)}, u32[]{:S(2)}) collective-permute-start(f32[2,32,1,128]{3,2,1,0:T(1,128)S(1)} %slice.116), channel_id=1, source_target_pairs={{0,1},{1,2},{2,3},{3,4},{4,5},{5,6},{6,7},{7,8},{8,9},{9,10},{10,1... | collective-permute-start | bytes 98312 | tf_op jit(solution)/shard_map/ppermute | solution.py:17
  272.4 18.7 %collective-permute-start.7 = (f32[2,32,16,1]{3,2,1,0:T(8,128)S(1)}, f32[2,32,16,1]{3,2,1,0:T(8,128)S(1)}, u32[]{:S(2)}, u32[]{:S(2)}) collective-permute-start(f32[2,32,16,1]{3,2,1,0:T(8,128)S(1)} %slice.112), channel_id=1, source_target_pairs={{0,16},{16,32},{32,48},{48,64},{64,80},{80,96},{96,112},{112,128},... | collective-permute-start | bytes 12296 | tf_op jit(solution)/shard_map/ppermute | solution.py:11
where the time goes:
time: 387 us
  blocking collectives  285 us (74%)
  waiting for transfers between devices  54.9 us (14%)
  starting transfers between devices  39.4 us (10%)
  other arithmetic  4.62 us (1%)
    psum x2, blocking collectives, sum_squares(): return lax.psum(local_sum(field, field), ('lon', 'lat'))  192 us
    psum x1, blocking collectives, body(): step_size = norm_now / lax.psum(local_sum(direction, image), ('lon', 'lat'))  93.8 us
    ppermute x5, waiting for transfers between devices, from_behind(): lax.ppermute(x, axis, [(i, (i + by) % devices) for i in range(devices)])  54.9 us
    ppermute x5, starting transfers between devices, shifted(): return lax.ppermute(x, axis, pairs)  20.2 us
    ppermute x5, starting transfers between devices, from_behind(): lax.ppermute(x, axis, [(i, (i + by) % devices) for i in range(devices)])  19.2 us
  transfers between devices with their start and end apart: 10, of which 5 were waited for; matrix products, arithmetic and copies ran while one was open for 0% of the time, Pallas kernels for 0%

commit v1 on v0

v1 whole, which is shorter than its diff:
```python
import jax
import jax.numpy as jnp
from jax import lax
from jax.experimental import pallas as pl
from jax.experimental.pallas import tpu as pltpu
from jax.sharding import PartitionSpec as P

MESH = pl.DeviceIdType.MESH
HUB = 1
CHUNK = 4


def kernel(nlon, nlat, rhs, mask_in, levels_in, ed_in, nd_in, vd_in,
           w_out, z_out, coef0, coef1, coef2, coef3, coef4,
           bp, wp, maskv, levelsv, edv, ndv, vdv,
           ocp, edoc, ndp, ce, cw, cn, cs, cdp,
           col_out, col_in, wcol_out, wcol_in,
           row_out, row_in, crow_out, crow_in, wrow_out, wrow_in,
           part, hub_in, peer_in, total,
           in_sem, send_sem, recv_sem, hub_send, hub_recv):
    levels_n = mask_in.shape[0]
    rows = mask_in.shape[1]
    lanes = mask_in.shape[2]
    lon, lat = lax.axis_index("lon"), lax.axis_index("lat")
    east = {"lon": lax.rem(lon + 1, nlon)}
    west = {"lon": lax.rem(lon + nlon - 1, nlon)}
    north = {"lat": lax.rem(lat + 1, nlat)}
    south = {"lat": lax.rem(lat + nlat - 1, nlat)}
    is_hub = lat == HUB

    barrier = pltpu.get_barrier_semaphore()
    for target in (east, west, north, south):
        pl.semaphore_signal(barrier, 1, device_id=target, device_id_type=MESH)

    loads = [
        pltpu.make_async_copy(mask_in, maskv, in_sem.at[0]),
        pltpu.make_async_copy(levels_in, levelsv, in_sem.at[1]),
        pltpu.make_async_copy(ed_in, edv, in_sem.at[2]),
        pltpu.make_async_copy(nd_in, ndv, in_sem.at[3]),
        pltpu.make_async_copy(vd_in, vdv, in_sem.at[4]),
        pltpu.make_async_copy(rhs, bp.at[:, pl.ds(1, levels_n)], in_sem.at[5]),
    ]
    for load in loads:
        load.start()

    @pl.when(is_hub)
    def _():
        def tell_member(d, carry):
            pl.semaphore_signal(barrier, 1, device_id={"lat": lax.rem(lat + d, nlat)}, device_id_type=MESH)
            return carry

        lax.fori_loop(1, nlat, tell_member, 0)

        def tell_peer(d, carry):
            pl.semaphore_signal(barrier, 1, device_id={"lon": lax.rem(lon + d, nlon)}, device_id_type=MESH)
            return carry

        lax.fori_loop(1, nlon, tell_peer, 0)

    zero_plane = jnp.zeros((2, 1, rows, lanes), jnp.float32)
    bp[:, 0:1] = zero_plane
    bp[:, levels_n + 1:levels_n + 2] = zero_plane
    wp[:, 0:1] = zero_plane
    wp[:, levels_n + 1:levels_n + 2] = zero_plane
    ocp[levels_n:levels_n + 1] = zero_plane[0]
    cdp[0:1] = zero_plane[0]

    lane2 = lax.broadcasted_iota(jnp.int32, (rows, lanes), 1)
    row2 = lax.broadcasted_iota(jnp.int32, (rows, lanes), 0)
    first_lane, last_lane = lane2 == 0, lane2 == lanes - 1
    first_row, last_row = row2 == 0, row2 == rows - 1

    def pack(piece, at, place):
        shift = (place - at) % lanes
        return pltpu.roll(piece, shift, 1) if shift else piece

    loads[0].wait()
    loads[1].wait()
    for k in range(levels_n):
        ocp[k] = jnp.where((maskv[k] == 1) & (levelsv[...] > k), 1.0, 0.0)
    for load in loads[2:5]:
        load.wait()
    for k in range(levels_n):
        oc = ocp[k]
        edoc[k] = edv[k].astype(jnp.float32) * oc
        nd = ndv[k].astype(jnp.float32) * oc
        ndp[k] = nd
        cdp[k + 1] = vdv[k].astype(jnp.float32) * oc * ocp[k + 1]
        crow_out[0, k] = oc[0:1]
        crow_out[1, k] = nd[rows - 1:rows]
    loads[5].wait()

    first_col = jnp.zeros((rows, lanes), jnp.float32)
    last_col = jnp.zeros((rows, lanes), jnp.float32)
    for t in range(2):
        for k in range(levels_n):
            piece = bp[t, k + 1]
            place = t * levels_n + k
            here = lane2 == place
            first_col = jnp.where(here, pack(piece, 0, place), first_col)
            last_col = jnp.where(here, pack(piece, lanes - 1, place), last_col)
            row_out[0, t, k] = piece[0:1]
            row_out[1, t, k] = piece[rows - 1:rows]
    for k in range(levels_n):
        place = 2 * levels_n + k
        here = lane2 == place
        first_col = jnp.where(here, pack(ocp[k], 0, place), first_col)
        last_col = jnp.where(here, pack(edoc[k], lanes - 1, place), last_col)
    col_out[0] = first_col
    col_out[1] = last_col

    def send(source, target, slot, number, device):
        copy = pltpu.make_async_remote_copy(
            source.at[slot], target.at[slot], send_sem.at[number], recv_sem.at[number],
            device_id=device, device_id_type=MESH)
        copy.start()
        return copy

    pl.semaphore_wait(barrier, jnp.where(is_hub, nlon + 3, 5))

    first = [
        send(row_out, row_in, 0, 0, south),
        send(row_out, row_in, 1, 1, north),
        send(crow_out, crow_in, 0, 2, south),
        send(crow_out, crow_in, 1, 3, north),
        send(col_out, col_in, 0, 4, west),
        send(col_out, col_in, 1, 5, east),
    ]
    for copy in first:
        copy.wait()

    from_east, from_west = col_in[0], col_in[1]
    top = jnp.where(lat == nlat - 1, 0.0, 1.0)
    bottom = jnp.where(lat == 0, 0.0, 1.0)
    for k in range(levels_n):
        oc = ocp[k]
        place = 2 * levels_n + k
        ed, nd = edoc[k], ndp[k]
        oc_east = jnp.where(last_lane, pack(from_east, place, lanes - 1), pltpu.roll(oc, lanes - 1, 1))
        ed_west = jnp.where(first_lane, pack(from_west, place, 0), pltpu.roll(ed, 1, 1))
        oc_north = jnp.where(last_row, crow_in[0, k] * top, pltpu.roll(oc, rows - 1, 0))
        nd_south = jnp.where(first_row, crow_in[1, k] * bottom, pltpu.roll(nd, 1, 0))
        ce[k] = ed * oc_east
        cw[k] = ed_west * oc
        cn[k] = nd * oc_north
        cs[k] = nd_south * oc

    def sides(field, t, k, east_col, west_col, north_row, south_row):
        v = field[t, k + 1]
        place = t * levels_n + k
        v_east = jnp.where(last_lane, pack(east_col, place, lanes - 1), pltpu.roll(v, lanes - 1, 1))
        v_west = jnp.where(first_lane, pack(west_col, place, 0), pltpu.roll(v, 1, 1))
        v_north = jnp.where(last_row, north_row, pltpu.roll(v, rows - 1, 0))
        v_south = jnp.where(first_row, south_row, pltpu.roll(v, 1, 0))
        return v, v_east, v_west, v_north, v_south

    def diffuse(field, t, k, *halo):
        v, v_east, v_west, v_north, v_south = sides(field, t, k, *halo)
        return v, (
            (ce[k] * (v - v_east) + cw[k] * (v - v_west))
            + (cn[k] * (v - v_north) + cs[k] * (v - v_south))
            + (cdp[k + 1] * (v - field[t, k + 2]) + cdp[k] * (v - field[t, k]))
        )

    sums = []
    first_col = jnp.zeros((rows, lanes), jnp.float32)
    last_col = jnp.zeros((rows, lanes), jnp.float32)
    for t in range(2):
        s0 = s1 = s2 = jnp.zeros((rows, lanes), jnp.float32)
        for k in range(levels_n):
            v, w = diffuse(bp, t, k, from_east, from_west, row_in[0, t, k], row_in[1, t, k])
            wp[t, k + 1] = w
            w_out[t, k] = w
            s0, s1, s2 = s0 + v * v, s1 + v * w, s2 + w * w
            place = t * levels_n + k
            here = lane2 == place
            first_col = jnp.where(here, pack(w, 0, place), first_col)
            last_col = jnp.where(here, pack(w, lanes - 1, place), last_col)
            wrow_out[0, t, k] = w[0:1]
            wrow_out[1, t, k] = w[rows - 1:rows]
        sums.append([s0, s1, s2])
    wcol_out[0] = first_col
    wcol_out[1] = last_col
    second = [
        send(wrow_out, wrow_in, 0, 6, south),
        send(wrow_out, wrow_in, 1, 7, north),
        send(wcol_out, wcol_in, 0, 8, west),
        send(wcol_out, wcol_in, 1, 9, east),
    ]
    for copy in second:
        copy.wait()
    from_east, from_west = wcol_in[0], wcol_in[1]
    for t in range(2):
        s3 = jnp.zeros((rows, lanes), jnp.float32)
        for k in range(levels_n):
            w, z = diffuse(wp, t, k, from_east, from_west, wrow_in[0, t, k], wrow_in[1, t, k])
            z_out[t, k] = z
            s3 = s3 + w * z
        sums[t].append(s3)

    lane1 = lax.broadcasted_iota(jnp.int32, (1, lanes), 1)
    mine = jnp.zeros((1, lanes), jnp.float32)
    for t in range(2):
        for j in range(4):
            one = jnp.sum(jnp.sum(sums[t][j], axis=0, keepdims=True), axis=1, keepdims=True)
            mine = jnp.where(lane1 == t * 4 + j, one, mine)
    part[0] = mine

    @pl.when(jnp.logical_not(is_hub))
    def _():
        slot = lax.rem(lat - HUB + nlat, nlat)
        give = pltpu.make_async_remote_copy(
            part.at[0], hub_in.at[slot], hub_send.at[0], hub_recv.at[0],
            device_id={"lat": HUB}, device_id_type=MESH)
        give.start()
        give.wait_send()
        take = pltpu.make_async_copy(total.at[0], total.at[0], hub_recv.at[2])
        take.wait()

    @pl.when(is_hub)
    def _():
        members = hub_in.at[pl.ds(1, nlat - 1)]
        peers = peer_in.at[pl.ds(1, nlon - 1)]
        hub_in[0] = part[0]
        pltpu.make_async_copy(members, members, hub_recv.at[0]).wait()
        peer_in[0] = jnp.sum(hub_in[...], axis=0)

        def give_peer(d, carry):
            pltpu.make_async_remote_copy(
                peer_in.at[0], peer_in.at[d], hub_send.at[1], hub_recv.at[1],
                device_id={"lon": lax.rem(lon + d, nlon)}, device_id_type=MESH).start()
            return carry

        lax.fori_loop(1, nlon, give_peer, 0)
        pltpu.make_async_copy(peers, peers, hub_recv.at[1]).wait()
        total[0] = jnp.sum(peer_in[...], axis=0)

        def give_member(d, carry):
            pltpu.make_async_remote_copy(
                total.at[0], total.at[0], hub_send.at[2], hub_recv.at[2],
                device_id={"lat": lax.rem(lat + d, nlat)}, device_id_type=MESH).start()
            return carry

        lax.fori_loop(1, nlat, give_member, 0)
        pltpu.make_async_copy(peers, peers, hub_send.at[1]).wait()
        pltpu.make_async_copy(members, members, hub_send.at[2]).wait()

    got = total[0]
    for t in range(2):
        m0, l1, l2, l3 = [jnp.sum(jnp.where(lane1 == t * 4 + j, got, 0.0), axis=1, keepdims=True) for j in range(4)]
        c0 = l1 / m0
        a0 = m0 / (m0 + l1)
        spread = l2 - l1 * c0
        curve = l3 - c0 * (2.0 * l2 - c0 * l1)
        beta = a0 * a0 * spread / m0
        a1 = spread / (spread + curve - a0 * spread * (spread / m0))
        g = a0 * c0 + beta
        values = (a0 + a1 * g, -a1 * a0, a0 * c0 - a1 * g, a1 * a0 - a0 - a1 * g, a1 * a0)
        for coef, value in zip((coef0, coef1, coef2, coef3, coef4), values, strict=True):
            coef[t:t + 1] = jnp.broadcast_to(value, (1, lanes))


def solution(mesh):
    nlon, nlat = mesh.shape["lon"], mesh.shape["lat"]

    def body(rhs, sea_mask, levels, ed, nd, vd):
        tracers, nz, rows, lanes = rhs.shape
        field = (tracers, nz + 2, rows, lanes)
        block = (nz, rows, lanes)
        f32 = jnp.float32
        whole = pl.BlockSpec(memory_space=pltpu.VMEM)
        w, z, *coef = pl.pallas_call(
            lambda *refs: kernel(nlon, nlat, *refs),
            out_shape=(
                jax.ShapeDtypeStruct(rhs.shape, f32),
                jax.ShapeDtypeStruct(rhs.shape, f32),
            ) + (jax.ShapeDtypeStruct((tracers, lanes), f32),) * 5,
            in_specs=[pl.BlockSpec(memory_space=pltpu.HBM)] * 6,
            out_specs=(whole,) * 7,
            scratch_shapes=[
                pltpu.VMEM(field, f32), pltpu.VMEM(field, f32),
                pltpu.VMEM(block, jnp.int32), pltpu.VMEM((rows, lanes), jnp.int32),
                pltpu.VMEM(block, jnp.bfloat16), pltpu.VMEM(block, jnp.bfloat16), pltpu.VMEM(block, jnp.bfloat16),
                pltpu.VMEM((nz + 1, rows, lanes), f32), pltpu.VMEM(block, f32), pltpu.VMEM(block, f32),
                pltpu.VMEM(block, f32), pltpu.VMEM(block, f32), pltpu.VMEM(block, f32), pltpu.VMEM(block, f32),
                pltpu.VMEM((nz + 1, rows, lanes), f32),
                pltpu.VMEM((2, rows, lanes), f32), pltpu.VMEM((2, rows, lanes), f32),
                pltpu.VMEM((2, rows, lanes), f32), pltpu.VMEM((2, rows, lanes), f32),
                pltpu.VMEM((2, tracers, nz, 1, lanes), f32), pltpu.VMEM((2, tracers, nz, 1, lanes), f32),
                pltpu.VMEM((2, nz, 1, lanes), f32), pltpu.VMEM((2, nz, 1, lanes), f32),
                pltpu.VMEM((2, tracers, nz, 1, lanes), f32), pltpu.VMEM((2, tracers, nz, 1, lanes), f32),
                pltpu.VMEM((1, 1, lanes), f32), pltpu.VMEM((nlat, 1, lanes), f32),
                pltpu.VMEM((nlon, 1, lanes), f32), pltpu.VMEM((1, 1, lanes), f32),
                pltpu.SemaphoreType.DMA((6,)), pltpu.SemaphoreType.DMA((10,)), pltpu.SemaphoreType.DMA((10,)),
                pltpu.SemaphoreType.DMA((3,)), pltpu.SemaphoreType.DMA((3,)),
            ],
            compiler_params=pltpu.CompilerParams(collective_id=0, has_side_effects=True, vmem_limit_bytes=32 * 1024 * 1024),
        )(*[pltpu.with_memory_space_constraint(one, pltpu.HBM) for one in (rhs, sea_mask, levels, ed, nd, vd)])
        c = [one[:, None, None, :] for one in coef]
        return c[0] * rhs + c[1] * w, c[2] * rhs + c[3] * w + c[4] * z

    return jax.shard_map(
        body,
        mesh=mesh,
        in_specs=(
            P(None, None, "lat", "lon"),
            P(None, "lat", "lon"),
            P("lat", "lon"),
            P(None, "lat", "lon"),
            P(None, "lat", "lon"),
            P(None, "lat", "lon"),
        ),
        out_specs=(P(None, None, "lat", "lon"), P(None, None, "lat", "lon")),
        check_vma=False,
    )
```

time: 387 us -> 40.5 us (0.10)
  blocking collectives: 285 us -> 0 us
  waiting for transfers between devices: 54.9 us -> 0 us
  starting transfers between devices: 39.4 us -> 0 us
  Pallas kernels: 0 us -> 38.6 us
    psum x3 -> x0, blocking collectives: 285 us -> none  [the longest x2 192 us: sum_squares(): return lax.psum(local_sum(field, field), ('lon', 'lat'))]
    ppermute x10 -> x0, waiting for transfers between devices: 54.9 us -> none  [the longest x5 54.9 us: from_behind(): lax.ppermute(x, axis, [(i, (i + by) % devices) for i in range(devices)])]
    ppermute x10 -> x0, starting transfers between devices: 39.4 us -> none  [the longest x5 20.2 us: shifted(): return lax.ppermute(x, axis, pairs)]
    pallas_call x0 -> x1, Pallas kernels: none -> 38.6 us  [body(): pl.pallas_call(lambda *refs: kernel(nlon, nlat, *refs), out_shape=(jax.Sh...]
  transfers between devices with their start and end apart: 10 -> 0, of which waited for: 5 -> 0; matrix products, arithmetic and copies ran while one was open for 0% -> 0% of each run, Pallas kernels for 0% -> 0%
where the time goes in v1:
time: 40.5 us; the launch traced here: 40.4 us
  Pallas kernels  38.6 us (95%)
  other arithmetic  1.11 us (3%)
  between operations  0.66 us (2%)
    pallas_call x1, Pallas kernels, body(): pl.pallas_call(lambda *refs: kernel(nlon, nlat, *refs), out_shape=(jax.Sh...  38.6 us
    add x1, other arithmetic, body(): return (c[0] * rhs + c[1] * w, c[2] * rhs + c[3] * w + c[4] * z)  1.11 us

profile of v1, /device:TPU:1, one launch (start us, length us, event | category | flops | bytes accessed | tf_op | source)
XLA Modules:
  0.0 40.4 jit_solution(9747127311997254035)
XLA Ops:
  0.6 0.0 copy-start
  0.6 38.6 %shard_map.77 = (f32[2,32,16,128]{3,2,1,0:T(8,128)S(1)}, f32[2,32,16,128]{3,2,1,0:T(8,128)S(1)}, f32[2,128]{1,0:T(2,128)S(1)}, f32[2,128]{1,0:T(2,128)S(1)}, f32...) custom-call(f32[2,32,16,128]{3,2,1,0:T(8,128)} %refs_0_.1, s32[32,16,128]{2,1,0:T(8,128)} %refs_1_.1, ...), custom_call_target="tpu_custom_call" | custom-call | tf_op jit(solution)/shard_map/pallas_call | solution.py:272
  39.2 0.0 copy-done
  39.3 1.1 %multiply_add_fusion = (f32[2,32,16,128]{3,2,1,0:T(8,128)}, f32[2,32,16,128]{3,2,1,0:T(8,128)}) fusion(f32[2,32,16,128]{3,2,1,0:T(8,128)S(1)} %get-tuple-element.15, f32[2,32,16,128]{3,2,1,0:T(8,128)S(1)} %get-tuple-element.11, f32[2,32,16,128]{3,2,1,0:T(8,128)S(1)} %copy-done, f32[2,128]{1,0:T(2,128)S(1)} %get-tuple-element.14, ...), kind=kLoop, calls=%fused_computation | loop fusion | flops 1048576 | bytes 2626560 | tf_op jit(solution)/shard_map/add | solution.py:300
Async XLA Ops:
  0.6 38.6 %copy-start = (f32[2,32,16,128]{3,2,1,0:T(8,128)S(1)}, f32[2,32,16,128]{3,2,1,0:T(8,128)}, u32[]{:S(2)}) copy-start(f32[2,32,16,128]{3,2,1,0:T(8,128)} %refs_0_.1) | copy-start | bytes 1572868

commit v2 on v1

v2 whole, which is shorter than its diff:
```python
import jax
import jax.numpy as jnp
from jax import lax
from jax.experimental import pallas as pl
from jax.experimental.pallas import tpu as pltpu
from jax.sharding import PartitionSpec as P

MESH = pl.DeviceIdType.MESH
HUB = 1


def kernel(nlon, nlat, rhs, mask_in, levels_in, ed_in, nd_in, vd_in,
           w_out, z_out, coef0, coef1, coef2, coef3, coef4,
           bp, maskv, levelsv, edv, ndv, vdv,
           ocp, ce, cn, cd,
           col_out, from_east, from_west,
           row0_out, row15_out, from_north, from_south,
           corner_out, corner_in, wcol_out, wcol_west, wrow_out, wrow_south, zrow_north,
           part, hub_in, peer_in, total,
           in_sem, send_sem, recv_sem, hub_send, hub_recv):
    nz, rows, lanes = mask_in.shape
    lon, lat = lax.axis_index("lon"), lax.axis_index("lat")
    lon_east, lon_west = lax.rem(lon + 1, nlon), lax.rem(lon + nlon - 1, nlon)
    lat_north, lat_south = lax.rem(lat + 1, nlat), lax.rem(lat + nlat - 1, nlat)
    east, west = {"lon": lon_east}, {"lon": lon_west}
    north, south = {"lat": lat_north}, {"lat": lat_south}
    north_east = {"lon": lon_east, "lat": lat_north}
    north_west = {"lon": lon_west, "lat": lat_north}
    south_east = {"lon": lon_east, "lat": lat_south}
    south_west = {"lon": lon_west, "lat": lat_south}
    is_hub = lat == HUB

    barrier = pltpu.get_barrier_semaphore()
    for target in (east, west, north, south, north_east, north_west, south_east):
        pl.semaphore_signal(barrier, 1, device_id=target, device_id_type=MESH)

    loads = [
        pltpu.make_async_copy(mask_in, maskv, in_sem.at[0]),
        pltpu.make_async_copy(levels_in, levelsv, in_sem.at[1]),
        pltpu.make_async_copy(ed_in, edv, in_sem.at[2]),
        pltpu.make_async_copy(nd_in, ndv, in_sem.at[3]),
        pltpu.make_async_copy(vd_in, vdv, in_sem.at[4]),
        pltpu.make_async_copy(rhs, bp, in_sem.at[5]),
    ]
    for load in loads:
        load.start()

    @pl.when(is_hub)
    def _():
        def tell_member(d, carry):
            pl.semaphore_signal(barrier, 1, device_id={"lat": lax.rem(lat + d, nlat)}, device_id_type=MESH)
            return carry

        lax.fori_loop(1, nlat, tell_member, 0)

        def tell_peer(d, carry):
            pl.semaphore_signal(barrier, 1, device_id={"lon": lax.rem(lon + d, nlon)}, device_id_type=MESH)
            return carry

        lax.fori_loop(1, nlon, tell_peer, 0)

    lane2 = lax.broadcasted_iota(jnp.int32, (rows, lanes), 1)
    row2 = lax.broadcasted_iota(jnp.int32, (rows, lanes), 0)
    lane1 = lax.broadcasted_iota(jnp.int32, (1, lanes), 1)
    first_row, last_row = row2 == 0, row2 == rows - 1
    edge_lane, edge_lane1 = (lane2 == 0) | (lane2 == lanes - 1), (lane1 == 0) | (lane1 == lanes - 1)
    pair = lane2 // 2
    even, even1 = lane2 % 2 == 0, lane1 % 2 == 0
    zero = jnp.zeros((rows, lanes), jnp.float32)

    def turn(piece, shift, axis=1):
        shift = shift % piece.shape[axis]
        return pltpu.roll(piece, shift, axis) if shift else piece

    def pack(piece, j, into):
        return jnp.where(pair == j, turn(piece, 2 * j + 1), into)

    def unpack(packed, j):
        return jnp.where(edge_lane, turn(packed, -1 - 2 * j), 0.0)

    def facing(east_packed, west_packed):
        return jnp.where(even if east_packed.shape[0] == rows else even1, turn(east_packed, -1), turn(west_packed, 1))

    def both(packed):
        return packed + turn(packed, 2 * nz)

    loads[0].wait()
    loads[1].wait()
    for k in range(nz):
        ocp[k] = jnp.where((maskv[k] == 1) & (levelsv[...] > k), 1.0, 0.0)
    for load in loads[2:5]:
        load.wait()
    half_lane = lane2 < lanes - 1
    edge_coef, edge_nd = zero, zero
    for k in range(nz):
        oc = ocp[k]
        ed = edv[k].astype(jnp.float32) * oc
        nd = ndv[k].astype(jnp.float32) * oc
        ce[k] = jnp.where(half_lane, ed * turn(oc, -1), 0.0)
        cn[k] = jnp.where(last_row, 0.0, nd * turn(oc, -1, 0))
        if k < nz - 1:
            cd[k] = vdv[k].astype(jnp.float32) * oc * ocp[k + 1]
        row0_out[2, k] = oc[0:1]
        row15_out[2, k] = nd[rows - 1:rows]
        edge_coef = jnp.where(pair == k, jnp.where(even, turn(ed, 2 * k + 1), turn(oc, 2 * k + 1)), edge_coef)
        edge_nd = pack(nd, k, edge_nd)
    edge_coef, edge_nd = both(edge_coef), both(edge_nd)
    loads[5].wait()

    sums = []
    edge_b, edge_p = zero, zero
    for t in range(2):
        s0 = zero
        down_above = zero
        for k in range(nz):
            v = bp[t, k]
            flow_east = ce[k] * (v - turn(v, -1))
            flow_north = cn[k] * (v - turn(v, -1, 0))
            inner = (flow_east - turn(flow_east, 1)) + (flow_north - turn(flow_north, 1, 0))
            if k < nz - 1:
                down = cd[k] * (v - bp[t, k + 1])
                inner = inner + (down - down_above)
                down_above = down
            else:
                inner = inner - down_above
            w_out[t, k] = inner
            s0 = s0 + v * v
            j = t * nz + k
            edge_b, edge_p = pack(v, j, edge_b), pack(inner, j, edge_p)
            row0_out[t, k] = v[0:1]
            row0_out[3 + t, k] = inner[0:1]
            row15_out[t, k] = v[rows - 1:rows]
        sums.append([s0])
    col_out[0], col_out[1], col_out[2], col_out[3] = edge_b, edge_coef, edge_p, edge_nd
    corner_out[0, 0], corner_out[0, 1] = edge_b[0:1], edge_coef[0:1]
    corner_out[1, 0], corner_out[1, 1] = edge_b[rows - 1:rows], edge_nd[rows - 1:rows]

    pl.semaphore_wait(barrier, jnp.where(is_hub, nlon + 6, 8))

    def send(source, target, number, device):
        copy = pltpu.make_async_remote_copy(
            source, target, send_sem.at[number], recv_sem.at[number], device_id=device, device_id_type=MESH)
        copy.start()
        return copy

    halo = [
        send(col_out, from_east, 0, west),
        send(col_out.at[pl.ds(0, 2)], from_west, 1, east),
        send(corner_out.at[0], corner_in.at[1], 2, south_west),
        send(corner_out.at[0], corner_in.at[2], 3, south_east),
        send(corner_out.at[1], corner_in.at[3], 4, north_west),
        send(corner_out.at[0], corner_in.at[0], 5, south),
        send(row0_out, from_north, 6, south),
        send(row15_out, from_south, 7, north),
    ]
    for copy in halo:
        copy.wait()

    top = jnp.where(lat == nlat - 1, 0.0, 1.0)
    bottom = jnp.where(lat == 0, 0.0, 1.0)
    cross = edge_coef * facing(from_east[1], from_west[1])
    faced_b = facing(from_east[0], from_west[0])
    flow = cross * (edge_b - faced_b)
    ghost = turn(from_east[2], -1) - flow
    ne_b, ne_oc = turn(corner_in[1, 0], -1), turn(corner_in[1, 1], -1)
    se_b, se_nd = turn(corner_in[3, 0], -1), turn(corner_in[3, 1], -1)
    east_oc, east_nd = turn(from_east[1], -1), turn(from_east[3], -1)
    ghost = ghost + jnp.where(last_row, (east_nd * (ne_oc * top)) * (faced_b - ne_b), 0.0)
    ghost = ghost + jnp.where(first_row, (east_oc * (se_nd * bottom)) * (faced_b - se_b), 0.0)
    flow_ghost = (corner_in[0, 1] * facing(corner_in[1, 1], corner_in[2, 1])) * (
        corner_in[0, 0] - facing(corner_in[1, 0], corner_in[2, 0]))

    edge_w = zero
    for t in range(2):
        s1 = s2 = s3 = zero
        s3_row = jnp.zeros((1, lanes), jnp.float32)
        w_above = None
        for k in range(nz):
            v = bp[t, k]
            j = t * nz + k
            c_north = row15_out[2, k] * (from_north[2, k] * top)
            c_south = (from_south[2, k] * bottom) * row0_out[2, k]
            out_north = c_north * (row15_out[t, k] - from_north[t, k])
            out_south = c_south * (row0_out[t, k] - from_south[t, k])
            w = w_out[t, k] + unpack(flow, j)
            w = w + jnp.where(last_row, out_north, jnp.where(first_row, out_south, 0.0))
            w_out[t, k] = w
            s1, s2 = s1 + v * w, s2 + w * w
            gap_east, gap_north = w - turn(w, -1), w - turn(w, -1, 0)
            s3 = s3 + (ce[k] * gap_east) * gap_east + (cn[k] * gap_north) * gap_north
            if k > 0:
                gap_down = w_above - w
                s3 = s3 + (cd[k - 1] * gap_down) * gap_down
            w_above = w
            edge_w = pack(w, j, edge_w)
            w_north = from_north[3 + t, k] - out_north + jnp.where(edge_lane1, turn(flow_ghost, -1 - 2 * j), 0.0)
            gap = w[rows - 1:rows] - w_north
            out_north = c_north * gap
            zrow_north[t, k] = out_north
            s3_row = s3_row + out_north * gap
            wrow_out[t, k] = w[rows - 1:rows]
        sums[t] += [s1, s2, s3 + jnp.where(first_row, s3_row, 0.0)]
    wcol_out[...] = edge_w
    later = [
        send(wcol_out, wcol_west, 8, east),
        send(wrow_out, wrow_south, 9, north),
    ]
    gap = edge_w - ghost
    east_sum = jnp.where(even, (cross * gap) * gap, 0.0)
    for t in range(2):
        sums[t][3] = sums[t][3] + jnp.where(lane2 // (2 * nz) == t, east_sum, 0.0)

    mine = jnp.zeros((1, lanes), jnp.float32)
    for t in range(2):
        for j in range(4):
            one = jnp.sum(jnp.sum(sums[t][j], axis=0, keepdims=True), axis=1, keepdims=True)
            mine = jnp.where(lane1 == t * 4 + j, one, mine)
    part[0] = mine

    @pl.when(jnp.logical_not(is_hub))
    def _():
        slot = lax.rem(lat - HUB + nlat, nlat)
        give = pltpu.make_async_remote_copy(
            part.at[0], hub_in.at[slot], hub_send.at[0], hub_recv.at[0],
            device_id={"lat": HUB}, device_id_type=MESH)
        give.start()
        give.wait_send()
    for copy in later:
        copy.wait()
    flow = cross * (edge_w - jnp.where(even, ghost, turn(wcol_west[...], 1)))
    for t in range(2):
        down_above = zero
        for k in range(nz):
            w = w_out[t, k]
            j = t * nz + k
            c_south = (from_south[2, k] * bottom) * row0_out[2, k]
            out_south = c_south * (w[0:1] - wrow_south[t, k])
            flow_east = ce[k] * (w - turn(w, -1))
            flow_north = cn[k] * (w - turn(w, -1, 0))
            z = (flow_east - turn(flow_east, 1)) + (flow_north - turn(flow_north, 1, 0))
            if k < nz - 1:
                down = cd[k] * (w - w_out[t, k + 1])
                z = z + (down - down_above)
                down_above = down
            else:
                z = z - down_above
            z = z + unpack(flow, j)
            z_out[t, k] = z + jnp.where(last_row, zrow_north[t, k], jnp.where(first_row, out_south, 0.0))

    @pl.when(jnp.logical_not(is_hub))
    def _():
        pltpu.make_async_copy(total.at[0], total.at[0], hub_recv.at[2]).wait()

    @pl.when(is_hub)
    def _():
        members = hub_in.at[pl.ds(1, nlat - 1)]
        peers = peer_in.at[pl.ds(1, nlon - 1)]
        hub_in[0] = part[0]
        pltpu.make_async_copy(members, members, hub_recv.at[0]).wait()
        peer_in[0] = jnp.sum(hub_in[...], axis=0)

        def give_peer(d, carry):
            pltpu.make_async_remote_copy(
                peer_in.at[0], peer_in.at[d], hub_send.at[1], hub_recv.at[1],
                device_id={"lon": lax.rem(lon + d, nlon)}, device_id_type=MESH).start()
            return carry

        lax.fori_loop(1, nlon, give_peer, 0)
        pltpu.make_async_copy(peers, peers, hub_recv.at[1]).wait()
        total[0] = jnp.sum(peer_in[...], axis=0)

        def give_member(d, carry):
            pltpu.make_async_remote_copy(
                total.at[0], total.at[0], hub_send.at[2], hub_recv.at[2],
                device_id={"lat": lax.rem(lat + d, nlat)}, device_id_type=MESH).start()
            return carry

        lax.fori_loop(1, nlat, give_member, 0)
        pltpu.make_async_copy(peers, peers, hub_send.at[1]).wait()
        pltpu.make_async_copy(members, members, hub_send.at[2]).wait()

    got = total[0]
    for t in range(2):
        m0, l1, l2, l3 = [jnp.sum(jnp.where(lane1 == t * 4 + j, got, 0.0), axis=1, keepdims=True) for j in range(4)]
        c0 = l1 / m0
        a0 = m0 / (m0 + l1)
        spread = l2 - l1 * c0
        curve = l3 - c0 * (2.0 * l2 - c0 * l1)
        beta = a0 * a0 * spread / m0
        a1 = spread / (spread + curve - a0 * spread * (spread / m0))
        g = a0 * c0 + beta
        values = (a0 + a1 * g, -a1 * a0, a0 * c0 - a1 * g, a1 * a0 - a0 - a1 * g, a1 * a0)
        for coef, value in zip((coef0, coef1, coef2, coef3, coef4), values, strict=True):
            coef[t:t + 1] = jnp.broadcast_to(value, (1, lanes))


def solution(mesh):
    nlon, nlat = mesh.shape["lon"], mesh.shape["lat"]

    def body(rhs, sea_mask, levels, ed, nd, vd):
        tracers, nz, rows, lanes = rhs.shape
        block = (nz, rows, lanes)
        f32 = jnp.float32
        whole = pl.BlockSpec(memory_space=pltpu.VMEM)
        w, z, *coef = pl.pallas_call(
            lambda *refs: kernel(nlon, nlat, *refs),
            out_shape=(
                jax.ShapeDtypeStruct(rhs.shape, f32),
                jax.ShapeDtypeStruct(rhs.shape, f32),
            ) + (jax.ShapeDtypeStruct((tracers, lanes), f32),) * 5,
            in_specs=[pl.BlockSpec(memory_space=pltpu.HBM)] * 6,
            out_specs=(whole,) * 7,
            scratch_shapes=[
                pltpu.VMEM(rhs.shape, f32),
                pltpu.VMEM(block, jnp.int32), pltpu.VMEM((rows, lanes), jnp.int32),
                pltpu.VMEM(block, jnp.bfloat16), pltpu.VMEM(block, jnp.bfloat16), pltpu.VMEM(block, jnp.bfloat16),
                pltpu.VMEM(block, f32),
                pltpu.VMEM(block, f32), pltpu.VMEM(block, f32), pltpu.VMEM(block, f32),
                pltpu.VMEM((4, rows, lanes), f32), pltpu.VMEM((4, rows, lanes), f32), pltpu.VMEM((2, rows, lanes), f32),
                pltpu.VMEM((5, nz, 1, lanes), f32), pltpu.VMEM((3, nz, 1, lanes), f32),
                pltpu.VMEM((5, nz, 1, lanes), f32), pltpu.VMEM((3, nz, 1, lanes), f32),
                pltpu.VMEM((2, 2, 1, lanes), f32), pltpu.VMEM((4, 2, 1, lanes), f32),
                pltpu.VMEM((rows, lanes), f32), pltpu.VMEM((rows, lanes), f32),
                pltpu.VMEM((2, nz, 1, lanes), f32), pltpu.VMEM((2, nz, 1, lanes), f32), pltpu.VMEM((2, nz, 1, lanes), f32),
                pltpu.VMEM((1, 1, lanes), f32), pltpu.VMEM((nlat, 1, lanes), f32),
                pltpu.VMEM((nlon, 1, lanes), f32), pltpu.VMEM((1, 1, lanes), f32),
                pltpu.SemaphoreType.DMA((6,)), pltpu.SemaphoreType.DMA((10,)), pltpu.SemaphoreType.DMA((10,)),
                pltpu.SemaphoreType.DMA((3,)), pltpu.SemaphoreType.DMA((3,)),
            ],
            compiler_params=pltpu.CompilerParams(collective_id=0, has_side_effects=True, vmem_limit_bytes=32 * 1024 * 1024),
        )(*[pltpu.with_memory_space_constraint(one, pltpu.HBM) for one in (rhs, sea_mask, levels, ed, nd, vd)])
        c = [one[:, None, None, :] for one in coef]
        return c[0] * rhs + c[1] * w, c[2] * rhs + c[3] * w + c[4] * z

    return jax.shard_map(
        body,
        mesh=mesh,
        in_specs=(
            P(None, None, "lat", "lon"),
            P(None, "lat", "lon"),
            P("lat", "lon"),
            P(None, "lat", "lon"),
            P(None, "lat", "lon"),
            P(None, "lat", "lon"),
        ),
        out_specs=(P(None, None, "lat", "lon"), P(None, None, "lat", "lon")),
        check_vma=False,
    )
```

time: 40.5 us -> 37.2 us (0.919)
  Pallas kernels: 38.6 us -> 35.3 us
    pallas_call x1, Pallas kernels: 38.6 us -> 35.3 us  [body(): pl.pallas_call(lambda *refs: kernel(nlon, nlat, *refs), out_shape=(jax.Sh...]
where the time goes in v2:
time: 37.2 us; the launch traced here: 37 us
  Pallas kernels  35.3 us (95%)
  other arithmetic  1.11 us (3%)
  between operations  0.66 us (2%)
    pallas_call x1, Pallas kernels, body(): pl.pallas_call(lambda *refs: kernel(nlon, nlat, *refs), out_shape=(jax.Sh...  35.3 us
    add x1, other arithmetic, body(): return (c[0] * rhs + c[1] * w, c[2] * rhs + c[3] * w + c[4] * z)  1.11 us

profile of v2, /device:TPU:1, one launch (start us, length us, event | category | flops | bytes accessed | tf_op | source)
XLA Modules:
  0.0 37.0 jit_solution(10031142848454452539)
XLA Ops:
  0.6 0.0 copy-start
  0.6 35.3 %shard_map.77 = (f32[2,32,16,128]{3,2,1,0:T(8,128)S(1)}, f32[2,32,16,128]{3,2,1,0:T(8,128)S(1)}, f32[2,128]{1,0:T(2,128)S(1)}, f32[2,128]{1,0:T(2,128)S(1)}, f32...) custom-call(f32[2,32,16,128]{3,2,1,0:T(8,128)} %refs_0_.1, s32[32,16,128]{2,1,0:T(8,128)} %refs_1_.1, ...), custom_call_target="tpu_custom_call" | custom-call | tf_op jit(solution)/shard_map/pallas_call | solution.py:305
  35.9 0.0 copy-done
  35.9 1.1 %multiply_add_fusion = (f32[2,32,16,128]{3,2,1,0:T(8,128)}, f32[2,32,16,128]{3,2,1,0:T(8,128)}) fusion(f32[2,32,16,128]{3,2,1,0:T(8,128)S(1)} %get-tuple-element.15, f32[2,32,16,128]{3,2,1,0:T(8,128)S(1)} %get-tuple-element.11, f32[2,32,16,128]{3,2,1,0:T(8,128)S(1)} %copy-done, f32[2,128]{1,0:T(2,128)S(1)} %get-tuple-element.14, ...), kind=kLoop, calls=%fused_computation | loop fusion | flops 1048576 | bytes 2626560 | tf_op jit(solution)/shard_map/add | solution.py:333
Async XLA Ops:
  0.6 35.3 %copy-start = (f32[2,32,16,128]{3,2,1,0:T(8,128)S(1)}, f32[2,32,16,128]{3,2,1,0:T(8,128)}, u32[]{:S(2)}) copy-start(f32[2,32,16,128]{3,2,1,0:T(8,128)} %refs_0_.1) | copy-start | bytes 1572868

commit v3 on v2

v3 whole, which is shorter than its diff:
```python
import jax
import jax.numpy as jnp
from jax import lax
from jax.experimental import pallas as pl
from jax.experimental.pallas import tpu as pltpu
from jax.sharding import PartitionSpec as P

MESH = pl.DeviceIdType.MESH
UNROLL = 4
HUB = 1


def kernel(nlon, nlat, rhs, mask_in, levels_in, ed_in, nd_in, vd_in,
           w_out, z_out, coef0, coef1, coef2, coef3, coef4,
           bp, maskv, levelsv, edv, ndv, vdv,
           ocp, edp, ndp, ce, cw, cn, cs, cd,
           col_out, from_east, from_west,
           row0_out, row15_out, from_north, from_south,
           corner_out, corner_in, wcol_out, wcol_west, wrow_out, wrow_south, zrow_north,
           part, hub_in, peer_in, total,
           in_sem, send_sem, recv_sem, hub_send, hub_recv):
    rows, lanes = levels_in.shape
    nz = mask_in.shape[0] // rows
    lon, lat = lax.axis_index("lon"), lax.axis_index("lat")
    lon_east, lon_west = lax.rem(lon + 1, nlon), lax.rem(lon + nlon - 1, nlon)
    lat_north, lat_south = lax.rem(lat + 1, nlat), lax.rem(lat + nlat - 1, nlat)
    east, west = {"lon": lon_east}, {"lon": lon_west}
    north, south = {"lat": lat_north}, {"lat": lat_south}
    north_east = {"lon": lon_east, "lat": lat_north}
    north_west = {"lon": lon_west, "lat": lat_north}
    south_east = {"lon": lon_east, "lat": lat_south}
    south_west = {"lon": lon_west, "lat": lat_south}
    is_hub = lat == HUB

    barrier = pltpu.get_barrier_semaphore()
    for target in (east, west, north, south, north_east, north_west, south_east):
        pl.semaphore_signal(barrier, 1, device_id=target, device_id_type=MESH)

    loads = [
        pltpu.make_async_copy(mask_in, maskv, in_sem.at[0]),
        pltpu.make_async_copy(levels_in, levelsv, in_sem.at[1]),
        pltpu.make_async_copy(ed_in, edv, in_sem.at[2]),
        pltpu.make_async_copy(nd_in, ndv, in_sem.at[3]),
        pltpu.make_async_copy(vd_in, vdv, in_sem.at[4]),
        pltpu.make_async_copy(rhs, bp, in_sem.at[5]),
    ]
    for load in loads:
        load.start()

    @pl.when(is_hub)
    def _():
        def tell_member(d, carry):
            pl.semaphore_signal(barrier, 1, device_id={"lat": lax.rem(lat + d, nlat)}, device_id_type=MESH)
            return carry

        lax.fori_loop(1, nlat, tell_member, 0)

        def tell_peer(d, carry):
            pl.semaphore_signal(barrier, 1, device_id={"lon": lax.rem(lon + d, nlon)}, device_id_type=MESH)
            return carry

        lax.fori_loop(1, nlon, tell_peer, 0)

    lane2 = lax.broadcasted_iota(jnp.int32, (rows, lanes), 1)
    row2 = lax.broadcasted_iota(jnp.int32, (rows, lanes), 0)
    lane1 = lax.broadcasted_iota(jnp.int32, (1, lanes), 1)
    lane_z = lax.broadcasted_iota(jnp.int32, (nz, lanes), 1)
    row_z = lax.broadcasted_iota(jnp.int32, (nz, lanes), 0)
    first_row, last_row = row2 == 0, row2 == rows - 1
    first_lane, last_lane = lane2 == 0, lane2 == lanes - 1
    edge_lane = first_lane | last_lane
    pair = lane2 // 2
    even, even1 = lane2 % 2 == 0, lane1 % 2 == 0
    zero = jnp.zeros((rows, lanes), jnp.float32)

    def at(k):
        return pl.ds(pl.multiple_of(k * rows, rows), rows)

    def over_levels(step, carry=0):
        def several(n, carry):
            for i in range(UNROLL):
                carry = step(n * UNROLL + i, carry)
            return carry

        return lax.fori_loop(0, nz // UNROLL, several, carry)

    row0, row15 = pl.ds(0, nz, stride=rows), pl.ds(rows - 1, nz, stride=rows)

    def turn(piece, shift, axis=1):
        if isinstance(shift, int):
            shift = shift % piece.shape[axis]
        return pltpu.roll(piece, shift, axis)

    def pack(piece, j, into):
        return jnp.where(pair == j, turn(piece, 2 * j + 1), into)

    def unpack(packed, j):
        return jnp.where(edge_lane, turn(packed, lanes - 1 - 2 * j), 0.0)

    def facing(east_packed, west_packed):
        return jnp.where(even if east_packed.shape[0] == rows else even1, turn(east_packed, -1), turn(west_packed, 1))

    def both(packed):
        return packed + turn(packed, 2 * nz)

    def inside(field, t, k):
        v = field[t, at(k)]
        flows = (ce[at(k)] * (v - turn(v, -1)) + cw[at(k)] * (v - turn(v, 1))) + (
            cn[at(k)] * (v - turn(v, -1, 0)) + cs[at(k)] * (v - turn(v, 1, 0)))
        below, above = field[t, at(jnp.minimum(k + 1, nz - 1))], field[t, at(jnp.maximum(k - 1, 0))]
        return v, flows + (cd[at(k + 1)] * (v - below) + cd[at(k)] * (v - above))

    loads[0].wait()
    loads[1].wait()
    @over_levels
    def _(k, carry):
        ocp[at(k)] = jnp.where((maskv[at(k)] == 1) & (levelsv[...] > k), 1.0, 0.0)
        return carry

    ocp[at(nz)] = zero
    cd[at(0)] = zero
    for load in loads[2:5]:
        load.wait()

    @over_levels
    def _(k, carry):
        oc = ocp[at(k)]
        edp[at(k)] = edv[at(k)].astype(jnp.float32) * oc
        ndp[at(k)] = ndv[at(k)].astype(jnp.float32) * oc
        cd[at(k + 1)] = vdv[at(k)].astype(jnp.float32) * oc * ocp[at(k + 1)]
        return carry

    def faces(k, carry):
        edge_coef, edge_nd = carry
        oc, ed, nd = ocp[at(k)], edp[at(k)], ndp[at(k)]
        ce[at(k)] = jnp.where(last_lane, 0.0, ed * turn(oc, -1))
        cw[at(k)] = jnp.where(first_lane, 0.0, turn(ed, 1) * oc)
        cn[at(k)] = jnp.where(last_row, 0.0, nd * turn(oc, -1, 0))
        cs[at(k)] = jnp.where(first_row, 0.0, turn(nd, 1, 0) * oc)
        return pack(jnp.where(last_lane, ed, oc), k, edge_coef), pack(nd, k, edge_nd)

    edge_coef, edge_nd = over_levels(faces, (zero, zero))
    edge_coef, edge_nd = both(edge_coef), both(edge_nd)
    row0_out[2] = ocp[row0]
    row15_out[2] = ndp[row15]
    loads[5].wait()

    def inner(k, carry):
        edge_b, edge_p, *squares = carry
        for t in range(2):
            v, flows = inside(bp, t, k)
            w_out[t, at(k)] = flows
            squares[t] = squares[t] + v * v
            j = t * nz + k
            edge_b, edge_p = pack(v, j, edge_b), pack(flows, j, edge_p)
        return edge_b, edge_p, *squares

    edge_b, edge_p, *squares = over_levels(inner, (zero,) * 4)
    sums = [[one] for one in squares]
    for t in range(2):
        row0_out[t] = bp[t, row0]
        row15_out[t] = bp[t, row15]
        row0_out[3 + t] = w_out[t, row0]
    col_out[0], col_out[1], col_out[2], col_out[3] = edge_b, edge_coef, edge_p, edge_nd
    corner_out[0, 0], corner_out[0, 1] = edge_b[0:1], edge_coef[0:1]
    corner_out[1, 0], corner_out[1, 1] = edge_b[rows - 1:rows], edge_nd[rows - 1:rows]

    pl.semaphore_wait(barrier, jnp.where(is_hub, nlon + 6, 8))

    def send(source, target, number, device):
        copy = pltpu.make_async_remote_copy(
            source, target, send_sem.at[number], recv_sem.at[number], device_id=device, device_id_type=MESH)
        copy.start()
        return copy

    halo = [
        send(col_out, from_east, 0, west),
        send(col_out.at[pl.ds(0, 2)], from_west, 1, east),
        send(corner_out.at[0], corner_in.at[1], 2, south_west),
        send(corner_out.at[0], corner_in.at[2], 3, south_east),
        send(corner_out.at[1], corner_in.at[3], 4, north_west),
        send(corner_out.at[0], corner_in.at[0], 5, south),
        send(row0_out, from_north, 6, south),
        send(row15_out, from_south, 7, north),
    ]
    for copy in halo:
        copy.wait()

    top = jnp.where(lat == nlat - 1, 0.0, 1.0)
    bottom = jnp.where(lat == 0, 0.0, 1.0)
    cross = edge_coef * facing(from_east[1], from_west[1])
    faced_b = facing(from_east[0], from_west[0])
    flow = cross * (edge_b - faced_b)
    ghost = turn(from_east[2], -1) - flow
    ne_b, ne_oc = turn(corner_in[1, 0], -1), turn(corner_in[1, 1], -1)
    se_b, se_nd = turn(corner_in[3, 0], -1), turn(corner_in[3, 1], -1)
    east_oc, east_nd = turn(from_east[1], -1), turn(from_east[3], -1)
    ghost = ghost + jnp.where(last_row, (east_nd * (ne_oc * top)) * (faced_b - ne_b), 0.0)
    ghost = ghost + jnp.where(first_row, (east_oc * (se_nd * bottom)) * (faced_b - se_b), 0.0)
    flow_ghost = (corner_in[0, 1] * facing(corner_in[1, 1], corner_in[2, 1])) * (
        corner_in[0, 0] - facing(corner_in[1, 0], corner_in[2, 0]))
    c_north = row15_out[2] * (from_north[2] * top)
    c_south = (from_south[2] * bottom) * row0_out[2]
    north_ghost = []
    for t in range(2):
        out_north = c_north * (row15_out[t] - from_north[t])
        w_out[t, row15] = w_out[t, row15] + out_north
        w_out[t, row0] = w_out[t, row0] + c_south * (row0_out[t] - from_south[t])
        place = 2 * (t * nz + row_z)
        spread_ghost = jnp.broadcast_to(flow_ghost, (nz, lanes))
        east_end = jnp.sum(jnp.where(lane_z == place, spread_ghost, 0.0), axis=1, keepdims=True)
        west_end = jnp.sum(jnp.where(lane_z == place + 1, spread_ghost, 0.0), axis=1, keepdims=True)
        ends = jnp.where(lane_z == lanes - 1, east_end, jnp.where(lane_z == 0, west_end, 0.0))
        north_ghost.append(from_north[3 + t] - out_north + ends)

    def complete(k, carry):
        edge_w, *dots = carry
        for t in range(2):
            v = bp[t, at(k)]
            j = t * nz + k
            w = w_out[t, at(k)] + unpack(flow, j)
            w_out[t, at(k)] = w
            dots[2 * t], dots[2 * t + 1] = dots[2 * t] + v * w, dots[2 * t + 1] + w * w
            edge_w = pack(w, j, edge_w)
        return edge_w, *dots

    edge_w, *dots = over_levels(complete, (zero,) * 5)
    for t in range(2):
        sums[t] += dots[2 * t:2 * t + 2]
        wrow_out[t] = w_out[t, row15]
    wcol_out[...] = edge_w
    later = [
        send(wcol_out, wcol_west, 8, east),
        send(wrow_out, wrow_south, 9, north),
    ]
    gap = edge_w - ghost
    east_sum = jnp.where(even, (cross * gap) * gap, 0.0)

    def energy(k, carry):
        carry = list(carry)
        for t in range(2):
            w = w_out[t, at(k)]
            gap_east, gap_north = w - turn(w, -1), w - turn(w, -1, 0)
            gap_down = w - w_out[t, at(jnp.minimum(k + 1, nz - 1))]
            carry[t] = carry[t] + (((ce[at(k)] * gap_east) * gap_east + (cn[at(k)] * gap_north) * gap_north)
                                   + (cd[at(k + 1)] * gap_down) * gap_down)
        return tuple(carry)

    cubes = over_levels(energy, tuple(jnp.where(lane2 // (2 * nz) == t, east_sum, 0.0) for t in range(2)))
    for t in range(2):
        s3 = cubes[t]
        gap = wrow_out[t] - north_ghost[t]
        out_north = c_north * gap
        zrow_north[t] = out_north
        row_sum = out_north * gap
        for k in range(nz // rows):
            s3 = s3 + row_sum[k * rows:(k + 1) * rows]
        sums[t].append(s3)

    mine = jnp.zeros((rows // 2, lanes), jnp.float32)
    for t in range(2):
        for j in range(4):
            one = jnp.sum(sums[t][j][:rows // 2] + sums[t][j][rows // 2:], axis=1, keepdims=True)
            mine = jnp.where(lane2[:rows // 2] == t * 4 + j, one, mine)
    mine = jnp.sum(mine, axis=0, keepdims=True)
    part[0] = mine

    @pl.when(jnp.logical_not(is_hub))
    def _():
        slot = lax.rem(lat - HUB + nlat, nlat)
        give = pltpu.make_async_remote_copy(
            part.at[0], hub_in.at[slot], hub_send.at[0], hub_recv.at[0],
            device_id={"lat": HUB}, device_id_type=MESH)
        give.start()
        give.wait_send()
    for copy in later:
        copy.wait()
    flow = cross * (edge_w - jnp.where(even, ghost, turn(wcol_west[...], 1)))

    @over_levels
    def _(k, carry):
        for t in range(2):
            z_out[t, at(k)] = inside(w_out, t, k)[1] + unpack(flow, t * nz + k)
        return carry

    for t in range(2):
        z_out[t, row15] = z_out[t, row15] + zrow_north[t]
        z_out[t, row0] = z_out[t, row0] + c_south * (w_out[t, row0] - wrow_south[t])

    @pl.when(jnp.logical_not(is_hub))
    def _():
        pltpu.make_async_copy(total.at[0], total.at[0], hub_recv.at[2]).wait()

    @pl.when(is_hub)
    def _():
        members = hub_in.at[pl.ds(1, nlat - 1)]
        peers = peer_in.at[pl.ds(1, nlon - 1)]
        hub_in[0] = part[0]
        pltpu.make_async_copy(members, members, hub_recv.at[0]).wait()
        peer_in[0] = jnp.sum(hub_in[...], axis=0)

        def give_peer(d, carry):
            pltpu.make_async_remote_copy(
                peer_in.at[0], peer_in.at[d], hub_send.at[1], hub_recv.at[1],
                device_id={"lon": lax.rem(lon + d, nlon)}, device_id_type=MESH).start()
            return carry

        lax.fori_loop(1, nlon, give_peer, 0)
        pltpu.make_async_copy(peers, peers, hub_recv.at[1]).wait()
        total[0] = jnp.sum(peer_in[...], axis=0)

        def give_member(d, carry):
            pltpu.make_async_remote_copy(
                total.at[0], total.at[0], hub_send.at[2], hub_recv.at[2],
                device_id={"lat": lax.rem(lat + d, nlat)}, device_id_type=MESH).start()
            return carry

        lax.fori_loop(1, nlat, give_member, 0)

    got = total[0]
    for t in range(2):
        m0, l1, l2, l3 = [jnp.sum(jnp.where(lane1 == t * 4 + j, got, 0.0), axis=1, keepdims=True) for j in range(4)]
        c0 = l1 / m0
        a0 = m0 / (m0 + l1)
        spread = l2 - l1 * c0
        curve = l3 - c0 * (2.0 * l2 - c0 * l1)
        beta = a0 * a0 * spread / m0
        a1 = spread / (spread + curve - a0 * spread * (spread / m0))
        g = a0 * c0 + beta
        values = (a0 + a1 * g, -a1 * a0, a0 * c0 - a1 * g, a1 * a0 - a0 - a1 * g, a1 * a0)
        for coef, value in zip((coef0, coef1, coef2, coef3, coef4), values, strict=True):
            coef[t:t + 1] = jnp.broadcast_to(value, (1, lanes))

    @pl.when(is_hub)
    def _():
        peers, members = peer_in.at[pl.ds(1, nlon - 1)], hub_in.at[pl.ds(1, nlat - 1)]
        pltpu.make_async_copy(peers, peers, hub_send.at[1]).wait()
        pltpu.make_async_copy(members, members, hub_send.at[2]).wait()


def solution(mesh):
    nlon, nlat = mesh.shape["lon"], mesh.shape["lat"]

    def body(rhs, sea_mask, levels, ed, nd, vd):
        tracers, nz, rows, lanes = rhs.shape
        field, block = (tracers, nz * rows, lanes), (nz * rows, lanes)
        taller = ((nz + 1) * rows, lanes)
        flat = [rhs.reshape(field), sea_mask.reshape(block), levels] + [one.reshape(block) for one in (ed, nd, vd)]
        f32 = jnp.float32
        whole = pl.BlockSpec(memory_space=pltpu.VMEM)
        w, z, *coef = pl.pallas_call(
            lambda *refs: kernel(nlon, nlat, *refs),
            out_shape=(
                jax.ShapeDtypeStruct(field, f32),
                jax.ShapeDtypeStruct(field, f32),
            ) + (jax.ShapeDtypeStruct((tracers, lanes), f32),) * 5,
            in_specs=[pl.BlockSpec(memory_space=pltpu.HBM)] * 6,
            out_specs=(whole,) * 7,
            scratch_shapes=[
                pltpu.VMEM(field, f32),
                pltpu.VMEM(block, jnp.int32), pltpu.VMEM((rows, lanes), jnp.int32),
                pltpu.VMEM(block, jnp.bfloat16), pltpu.VMEM(block, jnp.bfloat16), pltpu.VMEM(block, jnp.bfloat16),
                pltpu.VMEM(taller, f32), pltpu.VMEM(block, f32), pltpu.VMEM(block, f32),
                pltpu.VMEM(block, f32), pltpu.VMEM(block, f32), pltpu.VMEM(block, f32), pltpu.VMEM(block, f32),
                pltpu.VMEM(taller, f32),
                pltpu.VMEM((4, rows, lanes), f32), pltpu.VMEM((4, rows, lanes), f32), pltpu.VMEM((2, rows, lanes), f32),
                pltpu.VMEM((5, nz, lanes), f32), pltpu.VMEM((3, nz, lanes), f32),
                pltpu.VMEM((5, nz, lanes), f32), pltpu.VMEM((3, nz, lanes), f32),
                pltpu.VMEM((2, 2, 1, lanes), f32), pltpu.VMEM((4, 2, 1, lanes), f32),
                pltpu.VMEM((rows, lanes), f32), pltpu.VMEM((rows, lanes), f32),
                pltpu.VMEM((2, nz, lanes), f32), pltpu.VMEM((2, nz, lanes), f32), pltpu.VMEM((2, nz, lanes), f32),
                pltpu.VMEM((1, 1, lanes), f32), pltpu.VMEM((nlat, 1, lanes), f32),
                pltpu.VMEM((nlon, 1, lanes), f32), pltpu.VMEM((1, 1, lanes), f32),
                pltpu.SemaphoreType.DMA((6,)), pltpu.SemaphoreType.DMA((10,)), pltpu.SemaphoreType.DMA((10,)),
                pltpu.SemaphoreType.DMA((3,)), pltpu.SemaphoreType.DMA((3,)),
            ],
            compiler_params=pltpu.CompilerParams(collective_id=0, has_side_effects=True, vmem_limit_bytes=32 * 1024 * 1024),
        )(*[pltpu.with_memory_space_constraint(one, pltpu.HBM) for one in flat])
        w, z = w.reshape(rhs.shape), z.reshape(rhs.shape)
        c = [one[:, None, None, :] for one in coef]
        return c[0] * rhs + c[1] * w, c[2] * rhs + c[3] * w + c[4] * z

    return jax.shard_map(
        body,
        mesh=mesh,
        in_specs=(
            P(None, None, "lat", "lon"),
            P(None, "lat", "lon"),
            P("lat", "lon"),
            P(None, "lat", "lon"),
            P(None, "lat", "lon"),
            P(None, "lat", "lon"),
        ),
        out_specs=(P(None, None, "lat", "lon"), P(None, None, "lat", "lon")),
        check_vma=False,
    )
```

time: 37.2 us -> 34.9 us (0.938)
  Pallas kernels: 35.3 us -> 32.9 us
    pallas_call x1, Pallas kernels: 35.3 us -> 32.9 us  [body(): pl.pallas_call(lambda *refs: kernel(nlon, nlat, *refs), out_shape=(jax.Sh...]
where the time goes in v3:
time: 34.9 us; the launch traced here: 34.7 us
  Pallas kernels  32.9 us (94%)
  other arithmetic  1.11 us (3%)
  between operations  0.66 us (2%)
    pallas_call x1, Pallas kernels, body(): pl.pallas_call(lambda *refs: kernel(nlon, nlat, *refs), out_shape=(jax.Sh...  32.9 us
    add x1, other arithmetic, body(): return (c[0] * rhs + c[1] * w, c[2] * rhs + c[3] * w + c[4] * z)  1.11 us

profile of v3, /device:TPU:1, one launch (start us, length us, event | category | flops | bytes accessed | tf_op | source)
XLA Modules:
  0.0 34.7 jit_solution(8442690413110689245)
XLA Ops:
  0.6 0.0 copy-start
  0.6 32.9 %shard_map.77 = (f32[2,512,128]{2,1,0:T(8,128)S(1)}, f32[2,512,128]{2,1,0:T(8,128)S(1)}, f32[2,128]{1,0:T(2,128)S(1)}, f32[2,128]{1,0:T(2,128)S(1)}, f32[2,128]{...) custom-call(f32[2,512,128]{2,1,0:T(8,128)} %bitcast.9, s32[512,128]{1,0:T(8,128)} %bitcast.10, ...), custom_call_target="tpu_custom_call" | custom-call | tf_op jit(solution)/shard_map/pallas_call | solution.py:351
  33.6 0.0 copy-done
  33.6 1.1 %multiply_add_fusion = (f32[2,32,16,128]{3,2,1,0:T(8,128)}, f32[2,32,16,128]{3,2,1,0:T(8,128)}) fusion(f32[2,32,16,128]{3,2,1,0:T(8,128)S(1)} %bitcast.8, f32[2,32,16,128]{3,2,1,0:T(8,128)S(1)} %bitcast.7, f32[2,32,16,128]{3,2,1,0:T(8,128)S(1)} %copy-done, f32[2,128]{1,0:T(2,128)S(1)} %get-tuple-element.14, f32[2,128]{1,0:T(2,128)S(1)} %get-tuple-element.13, ...), kind=kLoop, calls=%fused_computation | loop fusion | flops 1048576 | bytes 2626560 | tf_op jit(solution)/shard_map/add | solution.py:381
Async XLA Ops:
  0.6 33.0 %copy-start = (f32[2,32,16,128]{3,2,1,0:T(8,128)S(1)}, f32[2,32,16,128]{3,2,1,0:T(8,128)}, u32[]{:S(2)}) copy-start(f32[2,32,16,128]{3,2,1,0:T(8,128)} %param.6) | copy-start | bytes 1572868

commit v4 on v3

--- a/solution.py
+++ b/solution.py
@@ -6,7 +6,7 @@
 from jax.sharding import PartitionSpec as P
 
 MESH = pl.DeviceIdType.MESH
-UNROLL = 4
+UNROLL = 16
 HUB = 1
 
 
@@ -184,7 +184,7 @@
         send(row15_out, from_south, 7, north),
     ]
     for copy in halo:
-        copy.wait()
+        copy.wait_recv()
 
     top = jnp.where(lat == nlat - 1, 0.0, 1.0)
     bottom = jnp.where(lat == 0, 0.0, 1.0)
@@ -274,7 +274,7 @@
         give.start()
         give.wait_send()
     for copy in later:
-        copy.wait()
+        copy.wait_recv()
     flow = cross * (edge_w - jnp.where(even, ghost, turn(wcol_west[...], 1)))
 
     @over_levels
@@ -330,6 +330,9 @@
         values = (a0 + a1 * g, -a1 * a0, a0 * c0 - a1 * g, a1 * a0 - a0 - a1 * g, a1 * a0)
         for coef, value in zip((coef0, coef1, coef2, coef3, coef4), values, strict=True):
             coef[t:t + 1] = jnp.broadcast_to(value, (1, lanes))
+
+    for copy in halo + later:
+        copy.wait_send()
 
     @pl.when(is_hub)
     def _():

time: 34.9 us -> 33.7 us (0.966)
  Pallas kernels: 32.9 us -> 31.8 us
    pallas_call x1, Pallas kernels: 32.9 us -> 31.8 us  [body(): pl.pallas_call(lambda *refs: kernel(nlon, nlat, *refs), out_shape=(jax.Sh...]
where the time goes in v4:
time: 33.7 us; the launch traced here: 33.5 us
  Pallas kernels  31.8 us (94%)
  other arithmetic  1.11 us (3%)
  between operations  0.66 us (2%)
    pallas_call x1, Pallas kernels, body(): pl.pallas_call(lambda *refs: kernel(nlon, nlat, *refs), out_shape=(jax.Sh...  31.8 us
    add x1, other arithmetic, body(): return (c[0] * rhs + c[1] * w, c[2] * rhs + c[3] * w + c[4] * z)  1.11 us

profile of v4, /device:TPU:1, one launch (start us, length us, event | category | flops | bytes accessed | tf_op | source)
XLA Modules:
  0.0 33.5 jit_solution(10059983673272876167)
XLA Ops:
  0.6 0.0 copy-start
  0.6 31.8 %shard_map.77 = (f32[2,512,128]{2,1,0:T(8,128)S(1)}, f32[2,512,128]{2,1,0:T(8,128)S(1)}, f32[2,128]{1,0:T(2,128)S(1)}, f32[2,128]{1,0:T(2,128)S(1)}, f32[2,128]{...) custom-call(f32[2,512,128]{2,1,0:T(8,128)} %bitcast.9, s32[512,128]{1,0:T(8,128)} %bitcast.10, ...), custom_call_target="tpu_custom_call" | custom-call | tf_op jit(solution)/shard_map/pallas_call | solution.py:354
  32.4 0.0 copy-done
  32.4 1.1 %multiply_add_fusion = (f32[2,32,16,128]{3,2,1,0:T(8,128)}, f32[2,32,16,128]{3,2,1,0:T(8,128)}) fusion(f32[2,32,16,128]{3,2,1,0:T(8,128)S(1)} %bitcast.8, f32[2,32,16,128]{3,2,1,0:T(8,128)S(1)} %bitcast.7, f32[2,32,16,128]{3,2,1,0:T(8,128)S(1)} %copy-done, f32[2,128]{1,0:T(2,128)S(1)} %get-tuple-element.14, f32[2,128]{1,0:T(2,128)S(1)} %get-tuple-element.13, ...), kind=kLoop, calls=%fused_computation | loop fusion | flops 1048576 | bytes 2626560 | tf_op jit(solution)/shard_map/add | solution.py:384
Async XLA Ops:
  0.6 31.8 %copy-start = (f32[2,32,16,128]{3,2,1,0:T(8,128)S(1)}, f32[2,32,16,128]{3,2,1,0:T(8,128)}, u32[]{:S(2)}) copy-start(f32[2,32,16,128]{3,2,1,0:T(8,128)} %param.6) | copy-start | bytes 1572868

commit v5 on v4

--- a/solution.py
+++ b/solution.py
@@ -7,12 +7,13 @@
 
 MESH = pl.DeviceIdType.MESH
 UNROLL = 16
+PARTS = 2
 HUB = 1
 
 
 def kernel(nlon, nlat, rhs, mask_in, levels_in, ed_in, nd_in, vd_in,
-           w_out, z_out, coef0, coef1, coef2, coef3, coef4,
-           bp, maskv, levelsv, edv, ndv, vdv,
+           bp, w_out, z_out, coef0, coef1, coef2, coef3, coef4,
+           maskv, levelsv, edv, ndv, vdv,
            ocp, edp, ndp, ce, cw, cn, cs, cd,
            col_out, from_east, from_west,
            row0_out, row15_out, from_north, from_south,
@@ -299,23 +300,17 @@
         pltpu.make_async_copy(members, members, hub_recv.at[0]).wait()
         peer_in[0] = jnp.sum(hub_in[...], axis=0)
 
-        def give_peer(d, carry):
+        for d in range(1, nlon):
             pltpu.make_async_remote_copy(
                 peer_in.at[0], peer_in.at[d], hub_send.at[1], hub_recv.at[1],
                 device_id={"lon": lax.rem(lon + d, nlon)}, device_id_type=MESH).start()
-            return carry
-
-        lax.fori_loop(1, nlon, give_peer, 0)
         pltpu.make_async_copy(peers, peers, hub_recv.at[1]).wait()
         total[0] = jnp.sum(peer_in[...], axis=0)
 
-        def give_member(d, carry):
+        for d in range(1, nlat):
             pltpu.make_async_remote_copy(
                 total.at[0], total.at[0], hub_send.at[2], hub_recv.at[2],
-                device_id={"lat": lax.rem(lat + d, nlat)}, device_id_type=MESH).start()
-            return carry
-
-        lax.fori_loop(1, nlat, give_member, 0)
+                device_id={"lat": (HUB + d) % nlat}, device_id_type=MESH).start()
 
     got = total[0]
     for t in range(2):
@@ -341,6 +336,22 @@
         pltpu.make_async_copy(members, members, hub_send.at[2]).wait()
 
 
+def finish(b, w, z, coef0, coef1, coef2, coef3, coef4, x_out, r_out, x, r, sem):
+    part = b.shape[1] // PARTS
+    copies = []
+    for t in range(2):
+        one = slice(t, t + 1)
+        for n in range(PARTS):
+            at = (t, pl.ds(n * part, part))
+            x[at] = coef0[one] * b[at] + coef1[one] * w[at]
+            r[at] = (coef2[one] * b[at] + coef3[one] * w[at]) + coef4[one] * z[at]
+            for source, target in ((x, x_out), (r, r_out)):
+                copies.append(pltpu.make_async_copy(source.at[at], target.at[at], sem.at[len(copies)]))
+                copies[-1].start()
+    for copy in copies:
+        copy.wait()
+
+
 def solution(mesh):
     nlon, nlat = mesh.shape["lon"], mesh.shape["lat"]
 
@@ -351,16 +362,12 @@
         flat = [rhs.reshape(field), sea_mask.reshape(block), levels] + [one.reshape(block) for one in (ed, nd, vd)]
         f32 = jnp.float32
         whole = pl.BlockSpec(memory_space=pltpu.VMEM)
-        w, z, *coef = pl.pallas_call(
+        fields = pl.pallas_call(
             lambda *refs: kernel(nlon, nlat, *refs),
-            out_shape=(
-                jax.ShapeDtypeStruct(field, f32),
-                jax.ShapeDtypeStruct(field, f32),
-            ) + (jax.ShapeDtypeStruct((tracers, lanes), f32),) * 5,
+            out_shape=(jax.ShapeDtypeStruct(field, f32),) * 3 + (jax.ShapeDtypeStruct((tracers, lanes), f32),) * 5,
             in_specs=[pl.BlockSpec(memory_space=pltpu.HBM)] * 6,
-            out_specs=(whole,) * 7,
+            out_specs=(whole,) * 8,
             scratch_shapes=[
-                pltpu.VMEM(field, f32),
                 pltpu.VMEM(block, jnp.int32), pltpu.VMEM((rows, lanes), jnp.int32),
                 pltpu.VMEM(block, jnp.bfloat16), pltpu.VMEM(block, jnp.bfloat16), pltpu.VMEM(block, jnp.bfloat16),
                 pltpu.VMEM(taller, f32), pltpu.VMEM(block, f32), pltpu.VMEM(block, f32),
@@ -379,9 +386,16 @@
             ],
             compiler_params=pltpu.CompilerParams(collective_id=0, has_side_effects=True, vmem_limit_bytes=32 * 1024 * 1024),
         )(*[pltpu.with_memory_space_constraint(one, pltpu.HBM) for one in flat])
-        w, z = w.reshape(rhs.shape), z.reshape(rhs.shape)
-        c = [one[:, None, None, :] for one in coef]
-        return c[0] * rhs + c[1] * w, c[2] * rhs + c[3] * w + c[4] * z
+        in_place = pl.BlockSpec(memory_space=pltpu.HBM)
+        solved = pl.pallas_call(
+            finish,
+            out_shape=(jax.ShapeDtypeStruct(field, f32),) * 2,
+            in_specs=[whole] * 8,
+            out_specs=(in_place,) * 2,
+            scratch_shapes=[pltpu.VMEM(field, f32), pltpu.VMEM(field, f32), pltpu.SemaphoreType.DMA((4 * PARTS,))],
+            compiler_params=pltpu.CompilerParams(vmem_limit_bytes=16 * 1024 * 1024),
+        )(*fields)
+        return tuple(one.reshape(rhs.shape) for one in solved)
 
     return jax.shard_map(
         body,

time: 33.7 us -> 33.4 us (level)
  other arithmetic: 1.11 us -> 0 us
  Pallas kernels: 31.8 us -> 32.6 us
    add x1 -> x0, other arithmetic: 1.11 us -> none  [body(): return (c[0] * rhs + c[1] * w, c[2] * rhs + c[3] * w + c[4] * z)]
    pallas_call x0 -> x1, Pallas kernels: none -> 1.05 us  [body(): pl.pallas_call(finish, out_shape=(jax.ShapeDtypeStruct(field, f32),) * 2,...]
where the time goes in v5:
time: 33.4 us; the launch traced here: 33.2 us
  Pallas kernels  32.6 us (98%)
  between operations  0.64 us (2%)
    pallas_call x1, Pallas kernels, body(): pl.pallas_call(lambda *refs: kernel(nlon, nlat, *refs), out_shape=(jax.Sh...  31.5 us
    pallas_call x1, Pallas kernels, body(): pl.pallas_call(finish, out_shape=(jax.ShapeDtypeStruct(field, f32),) * 2,...  1.05 us

profile of v5, /device:TPU:1, one launch (start us, length us, event | category | flops | bytes accessed | tf_op | source)
XLA Modules:
  0.0 33.2 jit_solution(7710821292015727254)
XLA Ops:
  0.6 31.5 %shard_map.77 = (f32[2,512,128]{2,1,0:T(8,128)S(1)}, f32[2,512,128]{2,1,0:T(8,128)S(1)}, f32[2,512,128]{2,1,0:T(8,128)S(1)}, f32[2,128]{1,0:T(2,128)S(1)}, f32[2...) custom-call(f32[2,512,128]{2,1,0:T(8,128)} %bitcast.7, ...), custom_call_target="tpu_custom_call" | custom-call | tf_op jit(solution)/shard_map/pallas_call | solution.py:365
  32.2 1.0 %shard_map.78 = (f32[2,512,128]{2,1,0:T(8,128)}, f32[2,512,128]{2,1,0:T(8,128)}) custom-call(f32[2,512,128]{2,1,0:T(8,128)S(1)} %get-tuple-element.12.b, f32[2,512,128]{2,1,0:T(8,128)S(1)} %get-tuple-element.13.w, f32[2,512,128]{2,1,0:T(8,128)S(1)} %get-tuple-element.14.z, f32[2,128]{1,0:T(2,128)S(1)} %get-tuple-element.15.coef0, ...), custom_call_target="tpu_custom_call" | custom-call | tf_op jit(solution)/shard_map/pallas_call | solution.py:390

commit v6 on v5

--- a/solution.py
+++ b/solution.py
@@ -175,14 +175,14 @@
         return copy
 
     halo = [
-        send(col_out, from_east, 0, west),
-        send(col_out.at[pl.ds(0, 2)], from_west, 1, east),
         send(corner_out.at[0], corner_in.at[1], 2, south_west),
         send(corner_out.at[0], corner_in.at[2], 3, south_east),
         send(corner_out.at[1], corner_in.at[3], 4, north_west),
         send(corner_out.at[0], corner_in.at[0], 5, south),
         send(row0_out, from_north, 6, south),
         send(row15_out, from_south, 7, north),
+        send(col_out, from_east, 0, west),
+        send(col_out.at[pl.ds(0, 2)], from_west, 1, east),
     ]
     for copy in halo:
         copy.wait_recv()
@@ -230,10 +230,6 @@
         sums[t] += dots[2 * t:2 * t + 2]
         wrow_out[t] = w_out[t, row15]
     wcol_out[...] = edge_w
-    later = [
-        send(wcol_out, wcol_west, 8, east),
-        send(wrow_out, wrow_south, 9, north),
-    ]
     gap = edge_w - ghost
     east_sum = jnp.where(even, (cross * gap) * gap, 0.0)
 
@@ -274,6 +270,10 @@
             device_id={"lat": HUB}, device_id_type=MESH)
         give.start()
         give.wait_send()
+    later = [
+        send(wcol_out, wcol_west, 8, east),
+        send(wrow_out, wrow_south, 9, north),
+    ]
     for copy in later:
         copy.wait_recv()
     flow = cross * (edge_w - jnp.where(even, ghost, turn(wcol_west[...], 1)))

time: 33.4 us -> 33.4 us (level)
  no operation moved by 1% of the time
where the time goes in v6:
time: 33.4 us; the launch traced here: 33.2 us
  Pallas kernels  32.6 us (98%)
  between operations  0.64 us (2%)
    pallas_call x1, Pallas kernels, body(): pl.pallas_call(lambda *refs: kernel(nlon, nlat, *refs), out_shape=(jax.Sh...  31.5 us
    pallas_call x1, Pallas kernels, body(): pl.pallas_call(finish, out_shape=(jax.ShapeDtypeStruct(field, f32),) * 2,...  1.05 us

profile of v6, /device:TPU:1, one launch (start us, length us, event | category | flops | bytes accessed | tf_op | source)
XLA Modules:
  0.0 33.2 jit_solution(16700387185769102222)
XLA Ops:
  0.6 31.5 %shard_map.77 = (f32[2,512,128]{2,1,0:T(8,128)S(1)}, f32[2,512,128]{2,1,0:T(8,128)S(1)}, f32[2,512,128]{2,1,0:T(8,128)S(1)}, f32[2,128]{1,0:T(2,128)S(1)}, f32[2...) custom-call(f32[2,512,128]{2,1,0:T(8,128)} %bitcast.7, ...), custom_call_target="tpu_custom_call" | custom-call | tf_op jit(solution)/shard_map/pallas_call | solution.py:365
  32.2 1.0 %shard_map.78 = (f32[2,512,128]{2,1,0:T(8,128)}, f32[2,512,128]{2,1,0:T(8,128)}) custom-call(f32[2,512,128]{2,1,0:T(8,128)S(1)} %get-tuple-element.12.b, f32[2,512,128]{2,1,0:T(8,128)S(1)} %get-tuple-element.13.w, f32[2,512,128]{2,1,0:T(8,128)S(1)} %get-tuple-element.14.z, f32[2,128]{1,0:T(2,128)S(1)} %get-tuple-element.15.coef0, ...), custom_call_target="tpu_custom_call" | custom-call | tf_op jit(solution)/shard_map/pallas_call | solution.py:390

commit v7 on v6

--- a/solution.py
+++ b/solution.py
@@ -77,13 +77,13 @@
     def at(k):
         return pl.ds(pl.multiple_of(k * rows, rows), rows)
 
-    def over_levels(step, carry=0):
+    def over_levels(step, carry=0, unroll=UNROLL):
         def several(n, carry):
-            for i in range(UNROLL):
-                carry = step(n * UNROLL + i, carry)
+            for i in range(unroll):
+                carry = step(n * unroll + i, carry)
             return carry
 
-        return lax.fori_loop(0, nz // UNROLL, several, carry)
+        return lax.fori_loop(0, nz // unroll, several, carry)
 
     row0, row15 = pl.ds(0, nz, stride=rows), pl.ds(rows - 1, nz, stride=rows)
 
@@ -156,7 +156,7 @@
             edge_b, edge_p = pack(v, j, edge_b), pack(flows, j, edge_p)
         return edge_b, edge_p, *squares
 
-    edge_b, edge_p, *squares = over_levels(inner, (zero,) * 4)
+    edge_b, edge_p, *squares = over_levels(inner, (zero,) * 4, nz)
     sums = [[one] for one in squares]
     for t in range(2):
         row0_out[t] = bp[t, row0]

time: 33.4 us -> 33.8 us (1.012)
  Pallas kernels: 32.6 us -> 33.1 us
    pallas_call x1, Pallas kernels: 31.5 us -> 32 us  [body(): pl.pallas_call(lambda *refs: kernel(nlon, nlat, *refs), out_shape=(jax.Sh...]
where the time goes in v7:
time: 33.8 us; the launch traced here: 33.7 us
  Pallas kernels  33.1 us (98%)
  between operations  0.64 us (2%)
    pallas_call x1, Pallas kernels, body(): pl.pallas_call(lambda *refs: kernel(nlon, nlat, *refs), out_shape=(jax.Sh...  32 us
    pallas_call x1, Pallas kernels, body(): pl.pallas_call(finish, out_shape=(jax.ShapeDtypeStruct(field, f32),) * 2,...  1.05 us

profile of v7, /device:TPU:1, one launch (start us, length us, event | category | flops | bytes accessed | tf_op | source)
XLA Modules:
  0.0 33.7 jit_solution(3741852407860381994)
XLA Ops:
  0.6 32.0 %shard_map.77 = (f32[2,512,128]{2,1,0:T(8,128)S(1)}, f32[2,512,128]{2,1,0:T(8,128)S(1)}, f32[2,512,128]{2,1,0:T(8,128)S(1)}, f32[2,128]{1,0:T(2,128)S(1)}, f32[2...) custom-call(f32[2,512,128]{2,1,0:T(8,128)} %bitcast.7, ...), custom_call_target="tpu_custom_call" | custom-call | tf_op jit(solution)/shard_map/pallas_call | solution.py:365
  32.7 1.0 %shard_map.78 = (f32[2,512,128]{2,1,0:T(8,128)}, f32[2,512,128]{2,1,0:T(8,128)}) custom-call(f32[2,512,128]{2,1,0:T(8,128)S(1)} %get-tuple-element.12.b, f32[2,512,128]{2,1,0:T(8,128)S(1)} %get-tuple-element.13.w, f32[2,512,128]{2,1,0:T(8,128)S(1)} %get-tuple-element.14.z, f32[2,128]{1,0:T(2,128)S(1)} %get-tuple-element.15.coef0, ...), custom_call_target="tpu_custom_call" | custom-call | tf_op jit(solution)/shard_map/pallas_call | solution.py:390
